TPU v7x, 128 devices: a whole 4x4x4 slice. The times are simulated.
128 devices in a mesh: tok: 32 (over y, x, core), kv: 4 (over z).
Axes of the slice: x: 4, y: 4, z: 4, core: 2. Of those that a mesh axis runs over, the one named last changes fastest.
Arguments:
- queries: bfloat16 [8192, 8192], P('tok', 'kv'), may hold values from -12 to 12
- key_states: bfloat16 [8192, 1024], P('tok', 'kv'), may hold values from -12 to 12
- value_states: bfloat16 [8192, 1024], P('tok', 'kv'), may hold values from -6 to 6
- doc_lengths: int32 [16], replicated, may hold values from 1 to 4096, 8192 in all
- block_plan: int32 [32, 32], replicated, may hold values from 0 to 31, each once within a row
Outputs:
- attention_out: bfloat16 [8192, 8192], P(('tok', 'kv'))
- served_lse: float32 [64, 8192], P('kv', 'tok')
Inputs may be any that keep to these rules, and one draw needn't show every extreme that they name: `doc_lengths`: positive lengths that sum to 8192; the largest is exactly 4096. Every row of block_plan is a permutation of 0 to 31.
All inputs are finite; a program needn't handle non-finite values.
Results may differ from a plain program's by a relative error of at most 0.012.
The roundings to bfloat16 on the way count: a program that leaves them out, or rounds other values in their place, can miss the bound.
Values may be sent and summed in bfloat16 or wider, within the bound.
A program may use at most 64 MiB of HBM per device.

v0:
```python
from functools import partial
import math

import jax
import jax.numpy as jnp
from jax import lax
from jax.sharding import PartitionSpec as P

HEAD_DIM = 128


THETA = 500000.0
NEG = -1e30


def doc_layout(doc_lengths, token_index):
    doc_ends = jnp.cumsum(doc_lengths)
    passed = token_index[:, None] >= doc_ends[None, :]
    doc_ids = jnp.sum(passed.astype(jnp.int32), axis=1)
    starts = jnp.sum(jnp.where(passed, doc_lengths[None, :], 0), axis=1)
    return (doc_ids, token_index - starts)


def rotate(inputs, positions, heads):
    half_dim = HEAD_DIM // 2
    inv_freq = jnp.power(
        jnp.float32(THETA), -(jnp.arange(half_dim, dtype=jnp.float32) * 2.0 / HEAD_DIM)
    )
    angles = positions.astype(jnp.float32)[:, None] * inv_freq[None, :]
    cosine = jnp.cos(angles)[:, None, :]
    sine_val = jnp.sin(angles)[:, None, :]
    shaped = inputs.astype(jnp.float32).reshape(inputs.shape[0], heads, HEAD_DIM)
    leading = shaped[..., :half_dim]
    trailing = shaped[..., half_dim:]
    turned = jnp.concatenate(
        [leading * cosine - trailing * sine_val, trailing * cosine + leading * sine_val], axis=-1
    )
    return turned.reshape(inputs.shape[0], heads * HEAD_DIM).astype(jnp.bfloat16)


def attend_block(
    carry_state, query_rows, query_index, query_docs, key_rows, value_rows, key_index, key_docs
):
    row_max, row_sum, weighted = carry_state
    score_scale = 1.0 / math.sqrt(HEAD_DIM)
    scores = (
        jnp.einsum("rgqd,ngd->gqrn", query_rows, key_rows, preferred_element_type=jnp.float32)
        * score_scale
    )
    allowed = (
        (query_docs[:, None] == key_docs[None, :])
        & (key_index[None, :] <= query_index[:, None])
        & (key_index[None, :] >= 0)
    )
    scores = jnp.where(allowed, scores, NEG)
    new_max = jnp.maximum(row_max, jnp.max(scores, axis=-1))
    weights = jnp.where(allowed, jnp.exp(scores - new_max[..., None]), 0.0)
    factor = jnp.exp(row_max - new_max)
    row_sum = row_sum * factor + jnp.sum(weights, axis=-1)
    probs = weights.astype(jnp.bfloat16)
    weighted = weighted * factor[..., None] + jnp.einsum(
        "gqrn,ngd->gqrd", probs, value_rows, preferred_element_type=jnp.float32
    )
    return (new_max, row_sum, weighted)


def fold_keys(
    carry_state, piece, start, query_rows=None, query_index=None, query_docs=None, doc_lengths=None
):
    key_piece, value_piece = piece
    count = key_piece.shape[0]
    stride = math.gcd(count, 512)
    kv_local = key_piece.shape[1] // HEAD_DIM

    def inner(counter, running):
        offset = counter * stride
        key_rows = lax.dynamic_slice_in_dim(key_piece, offset, stride, 0).reshape(
            stride, kv_local, HEAD_DIM
        )
        value_rows = lax.dynamic_slice_in_dim(value_piece, offset, stride, 0).reshape(
            stride, kv_local, HEAD_DIM
        )
        key_index = offset + jnp.arange(stride, dtype=jnp.int32)
        key_docs, unused_pos = doc_layout(doc_lengths, key_index)
        return attend_block(
            running, query_rows, query_index, query_docs, key_rows, value_rows, key_index, key_docs
        )

    return lax.fori_loop(0, count // stride, inner, carry_state)


def finish(carry_state, rows, q_local):
    row_max, row_sum, weighted = carry_state
    mixed = weighted / row_sum[..., None]
    result = (
        jnp.transpose(mixed, (2, 0, 1, 3)).reshape(rows, q_local * HEAD_DIM).astype(jnp.bfloat16)
    )
    log_norm = (row_max + jnp.log(row_sum)).reshape(q_local, rows)
    return (result, log_norm)


def body(queries, key_states, value_states, doc_lengths, block_plan):
    shards = lax.axis_size("tok")
    shard_index = lax.axis_index("tok")
    tok_dev = queries.shape[0]
    block_rows = tok_dev // shards
    kv_local = key_states.shape[1] // HEAD_DIM
    q_local = queries.shape[1] // HEAD_DIM
    per_group = q_local // kv_local
    token_index = shard_index * tok_dev + jnp.arange(tok_dev, dtype=jnp.int32)
    doc_ids, positions = doc_layout(doc_lengths, token_index)
    q_rot = rotate(queries, positions, q_local)
    k_rot = rotate(key_states, positions, kv_local)
    my_blocks = lax.dynamic_index_in_dim(block_plan, shard_index, 0, keepdims=False)
    initial = (
        jnp.full((kv_local, per_group, tok_dev), NEG, jnp.float32),
        jnp.zeros((kv_local, per_group, tok_dev), jnp.float32),
        jnp.zeros((kv_local, per_group, tok_dev, HEAD_DIM), jnp.float32),
    )
    plan_column = lax.dynamic_index_in_dim(block_plan, shard_index, 1, keepdims=False)
    outgoing = jnp.take(q_rot.reshape(shards, block_rows, q_local * HEAD_DIM), my_blocks, axis=0)
    incoming = lax.all_to_all(outgoing, "tok", split_axis=0, concat_axis=0, tiled=True)
    served_index = (
        jnp.arange(shards, dtype=jnp.int32)[:, None] * tok_dev
        + plan_column[:, None] * block_rows
        + jnp.arange(block_rows, dtype=jnp.int32)[None, :]
    ).reshape(tok_dev)
    served_docs, unused_pos = doc_layout(doc_lengths, served_index)
    served_rows = incoming.reshape(tok_dev, kv_local, per_group, HEAD_DIM)
    folder = partial(
        fold_keys,
        query_rows=served_rows,
        query_index=served_index,
        query_docs=served_docs,
        doc_lengths=doc_lengths,
    )
    final_state = folder(
        initial,
        (
            lax.all_gather(k_rot, "tok", axis=0, tiled=True),
            lax.all_gather(value_states, "tok", axis=0, tiled=True),
        ),
        jnp.int32(0),
    )
    result, served_lse = finish(final_state, tok_dev, q_local)
    returned = lax.all_to_all(
        result.reshape(shards, block_rows, q_local * HEAD_DIM),
        "tok",
        split_axis=0,
        concat_axis=0,
        tiled=True,
    )
    ordered = (
        jnp.zeros_like(returned).at[my_blocks].set(returned).reshape(tok_dev, q_local * HEAD_DIM)
    )
    attention_out = lax.all_to_all(ordered, "kv", split_axis=0, concat_axis=1, tiled=True)
    return (attention_out, served_lse)


def solution(mesh):
    return jax.shard_map(
        body,
        mesh=mesh,
        in_specs=(P("tok", "kv"), P("tok", "kv"), P("tok", "kv"), P(), P()),
        out_specs=(P(("tok", "kv"), None), P("kv", "tok")),
        check_vma=False,
    )
```

profile of v0, /device:TPU:1, one launch (start us, length us, event | category | flops | bytes accessed | tf_op | source)
XLA Modules:
  0.0 487.6 jit_solution(9570828459599723917)
XLA Ops:
  7.2 1.6 add_reduce_fusion
  9.7 1.4 broadcast_in_dim.111
  11.0 1.3 select_reduce_fusion
  14.4 1.7 copy.36
  22.5 8.6 %all-to-all-start = ((bf16[32,8,2048]{2,1,0:T(8,128)(2,1)}), bf16[32,8,2048]{2,1,0:T(8,128)(2,1)S(1)}, u32[]{:S(2)}, u32[]{:S(2)}) async-start(bf16[32,8,2048]{2,1,0:T(8,128)(2,1)} %broadcast_select_fusion), calls=%async_computation | async-start | bytes 2097152 | tf_op jit(solution)/shard_map/all_to_all | solution.py:122
  31.1 18.3 %all-to-all-done = bf16[32,8,2048]{2,1,0:T(8,128)(2,1)S(1)} async-done(((bf16[32,8,2048]{2,1,0:T(8,128)(2,1)}), bf16[32,8,2048]{2,1,0:T(8,128)(2,1)S(1)}, u32[]{:S(2)}, u32[]{:S(2)}) %all-to-all-start) | async-done | bytes 1048608 | tf_op jit(solution)/shard_map/all_to_all | solution.py:122
  50.0 24.9 %all-gather.3.cloned.1.call-done = bf16[8192,256]{0,1:T(8,128)(2,1)} async-done(((bf16[256,256]{0,1:T(8,128)(2,1)}), bf16[8192,256]{0,1:T(8,128)(2,1)}) %all-gather.3.cloned.1.call-update) | async-done | bytes 4194320 | tf_op jit(solution)/shard_map/all_gather | solution.py:140
  74.9 50.9 %all-gather.5.cloned.1.call-done = bf16[8192,256]{0,1:T(8,128)(2,1)} async-done(((bf16[256,256]{0,1:T(8,128)(2,1)}), bf16[8192,256]{0,1:T(8,128)(2,1)}) %all-gather.5.cloned.1.call-update) | async-done | bytes 4194320 | tf_op jit(solution)/shard_map/all_gather | solution.py:141
  125.8 304.6 %while.20 = (s32[]{:T(128)}, f32[2,8,256]{2,1,0:T(8,128)S(1)}, f32[2,8,256]{2,1,0:T(8,128)}, f32[2,8,256,128]{3,2,1,0:T(8,128)S(1)}, s32[256]{0:T(256)}, /*index...) while((s32[]{:T(128)}, f32[2,8,256]{2,1,0:T(8,128)S(1)}, ...), condition=%wide.region_7.8_spmd.clone, body=%wide.region_3.7_spmd.clone.sunk | while | flops 1103148288 | bytes 66470364 | solution.py:89
  129.4 5.3 %fusion.32 = (f32[2,8,256]{2,1,0:T(8,128)}, f32[2,512,256,8]{2,1,3,0:T(8,128)}) fusion(pred[256,512]{0,1:T(8,128)(4,1)S(1)} %and_and_fusion.2, bf16[512,2,128,1]{0,2,3,1:T(8,128)(2,1)S(1)} %bitcast.72, bf16[256,2,8,128]{3,0,2,1:T(8,128)(2,1)S(1)} %get-tuple-element.448), kind=kOutput, calls=%fused_computation.5.clone.1 | convolution fusion | flops 543158272 | bytes 9846784 | tf_op jit(solution)/shard_map/while/body/eval_jaxpr/rgqd,ngd->gqrn/dot_general | solution.py:47
  135.4 4.6 fusion.33
  141.3 3.5 fusion.35
  148.4 5.3 %fusion.32 = (f32[2,8,256]{2,1,0:T(8,128)}, f32[2,512,256,8]{2,1,3,0:T(8,128)}) fusion(pred[256,512]{0,1:T(8,128)(4,1)S(1)} %and_and_fusion.2, bf16[512,2,128,1]{0,2,3,1:T(8,128)(2,1)S(1)} %bitcast.72, bf16[256,2,8,128]{3,0,2,1:T(8,128)(2,1)S(1)} %get-tuple-element.448), kind=kOutput, calls=%fused_computation.5.clone.1 | convolution fusion | flops 543158272 | bytes 9846784 | tf_op jit(solution)/shard_map/while/body/eval_jaxpr/rgqd,ngd->gqrn/dot_general | solution.py:47
  154.5 4.6 fusion.33
  160.3 3.5 fusion.35
  167.5 5.3 %fusion.32 = (f32[2,8,256]{2,1,0:T(8,128)}, f32[2,512,256,8]{2,1,3,0:T(8,128)}) fusion(pred[256,512]{0,1:T(8,128)(4,1)S(1)} %and_and_fusion.2, bf16[512,2,128,1]{0,2,3,1:T(8,128)(2,1)S(1)} %bitcast.72, bf16[256,2,8,128]{3,0,2,1:T(8,128)(2,1)S(1)} %get-tuple-element.448), kind=kOutput, calls=%fused_computation.5.clone.1 | convolution fusion | flops 543158272 | bytes 9846784 | tf_op jit(solution)/shard_map/while/body/eval_jaxpr/rgqd,ngd->gqrn/dot_general | solution.py:47
  173.5 4.6 fusion.33
  178.2 1.2 copy-done
  179.4 3.5 fusion.35
  186.5 5.3 %fusion.32 = (f32[2,8,256]{2,1,0:T(8,128)}, f32[2,512,256,8]{2,1,3,0:T(8,128)}) fusion(pred[256,512]{0,1:T(8,128)(4,1)S(1)} %and_and_fusion.2, bf16[512,2,128,1]{0,2,3,1:T(8,128)(2,1)S(1)} %bitcast.72, bf16[256,2,8,128]{3,0,2,1:T(8,128)(2,1)S(1)} %get-tuple-element.448), kind=kOutput, calls=%fused_computation.5.clone.1 | convolution fusion | flops 543158272 | bytes 9846784 | tf_op jit(solution)/shard_map/while/body/eval_jaxpr/rgqd,ngd->gqrn/dot_general | solution.py:47
  192.6 4.6 fusion.33
  197.2 1.2 copy-done
  198.4 3.5 fusion.35
  205.5 5.3 %fusion.32 = (f32[2,8,256]{2,1,0:T(8,128)}, f32[2,512,256,8]{2,1,3,0:T(8,128)}) fusion(pred[256,512]{0,1:T(8,128)(4,1)S(1)} %and_and_fusion.2, bf16[512,2,128,1]{0,2,3,1:T(8,128)(2,1)S(1)} %bitcast.72, bf16[256,2,8,128]{3,0,2,1:T(8,128)(2,1)S(1)} %get-tuple-element.448), kind=kOutput, calls=%fused_computation.5.clone.1 | convolution fusion | flops 543158272 | bytes 9846784 | tf_op jit(solution)/shard_map/while/body/eval_jaxpr/rgqd,ngd->gqrn/dot_general | solution.py:47
  211.6 4.6 fusion.33
  217.5 3.5 fusion.35
  224.6 5.3 %fusion.32 = (f32[2,8,256]{2,1,0:T(8,128)}, f32[2,512,256,8]{2,1,3,0:T(8,128)}) fusion(pred[256,512]{0,1:T(8,128)(4,1)S(1)} %and_and_fusion.2, bf16[512,2,128,1]{0,2,3,1:T(8,128)(2,1)S(1)} %bitcast.72, bf16[256,2,8,128]{3,0,2,1:T(8,128)(2,1)S(1)} %get-tuple-element.448), kind=kOutput, calls=%fused_computation.5.clone.1 | convolution fusion | flops 543158272 | bytes 9846784 | tf_op jit(solution)/shard_map/while/body/eval_jaxpr/rgqd,ngd->gqrn/dot_general | solution.py:47
  230.6 4.6 fusion.33
  236.5 3.5 fusion.35
  243.6 5.3 %fusion.32 = (f32[2,8,256]{2,1,0:T(8,128)}, f32[2,512,256,8]{2,1,3,0:T(8,128)}) fusion(pred[256,512]{0,1:T(8,128)(4,1)S(1)} %and_and_fusion.2, bf16[512,2,128,1]{0,2,3,1:T(8,128)(2,1)S(1)} %bitcast.72, bf16[256,2,8,128]{3,0,2,1:T(8,128)(2,1)S(1)} %get-tuple-element.448), kind=kOutput, calls=%fused_computation.5.clone.1 | convolution fusion | flops 543158272 | bytes 9846784 | tf_op jit(solution)/shard_map/while/body/eval_jaxpr/rgqd,ngd->gqrn/dot_general | solution.py:47
  249.7 4.6 fusion.33
  255.5 3.5 fusion.35
  262.7 5.3 %fusion.32 = (f32[2,8,256]{2,1,0:T(8,128)}, f32[2,512,256,8]{2,1,3,0:T(8,128)}) fusion(pred[256,512]{0,1:T(8,128)(4,1)S(1)} %and_and_fusion.2, bf16[512,2,128,1]{0,2,3,1:T(8,128)(2,1)S(1)} %bitcast.72, bf16[256,2,8,128]{3,0,2,1:T(8,128)(2,1)S(1)} %get-tuple-element.448), kind=kOutput, calls=%fused_computation.5.clone.1 | convolution fusion | flops 543158272 | bytes 9846784 | tf_op jit(solution)/shard_map/while/body/eval_jaxpr/rgqd,ngd->gqrn/dot_general | solution.py:47
  268.7 4.6 fusion.33
  274.6 3.5 fusion.35
  281.7 5.3 %fusion.32 = (f32[2,8,256]{2,1,0:T(8,128)}, f32[2,512,256,8]{2,1,3,0:T(8,128)}) fusion(pred[256,512]{0,1:T(8,128)(4,1)S(1)} %and_and_fusion.2, bf16[512,2,128,1]{0,2,3,1:T(8,128)(2,1)S(1)} %bitcast.72, bf16[256,2,8,128]{3,0,2,1:T(8,128)(2,1)S(1)} %get-tuple-element.448), kind=kOutput, calls=%fused_computation.5.clone.1 | convolution fusion | flops 543158272 | bytes 9846784 | tf_op jit(solution)/shard_map/while/body/eval_jaxpr/rgqd,ngd->gqrn/dot_general | solution.py:47
  287.8 4.6 fusion.33
  293.6 3.5 fusion.35
  300.7 5.3 %fusion.32 = (f32[2,8,256]{2,1,0:T(8,128)}, f32[2,512,256,8]{2,1,3,0:T(8,128)}) fusion(pred[256,512]{0,1:T(8,128)(4,1)S(1)} %and_and_fusion.2, bf16[512,2,128,1]{0,2,3,1:T(8,128)(2,1)S(1)} %bitcast.72, bf16[256,2,8,128]{3,0,2,1:T(8,128)(2,1)S(1)} %get-tuple-element.448), kind=kOutput, calls=%fused_computation.5.clone.1 | convolution fusion | flops 543158272 | bytes 9846784 | tf_op jit(solution)/shard_map/while/body/eval_jaxpr/rgqd,ngd->gqrn/dot_general | solution.py:47
  306.8 4.6 fusion.33
  312.7 3.5 fusion.35
  319.8 5.3 %fusion.32 = (f32[2,8,256]{2,1,0:T(8,128)}, f32[2,512,256,8]{2,1,3,0:T(8,128)}) fusion(pred[256,512]{0,1:T(8,128)(4,1)S(1)} %and_and_fusion.2, bf16[512,2,128,1]{0,2,3,1:T(8,128)(2,1)S(1)} %bitcast.72, bf16[256,2,8,128]{3,0,2,1:T(8,128)(2,1)S(1)} %get-tuple-element.448), kind=kOutput, calls=%fused_computation.5.clone.1 | convolution fusion | flops 543158272 | bytes 9846784 | tf_op jit(solution)/shard_map/while/body/eval_jaxpr/rgqd,ngd->gqrn/dot_general | solution.py:47
  325.8 4.6 fusion.33
  331.7 3.5 fusion.35
  338.8 5.3 %fusion.32 = (f32[2,8,256]{2,1,0:T(8,128)}, f32[2,512,256,8]{2,1,3,0:T(8,128)}) fusion(pred[256,512]{0,1:T(8,128)(4,1)S(1)} %and_and_fusion.2, bf16[512,2,128,1]{0,2,3,1:T(8,128)(2,1)S(1)} %bitcast.72, bf16[256,2,8,128]{3,0,2,1:T(8,128)(2,1)S(1)} %get-tuple-element.448), kind=kOutput, calls=%fused_computation.5.clone.1 | convolution fusion | flops 543158272 | bytes 9846784 | tf_op jit(solution)/shard_map/while/body/eval_jaxpr/rgqd,ngd->gqrn/dot_general | solution.py:47
  344.9 4.6 fusion.33
  350.7 3.5 fusion.35
  357.9 5.3 %fusion.32 = (f32[2,8,256]{2,1,0:T(8,128)}, f32[2,512,256,8]{2,1,3,0:T(8,128)}) fusion(pred[256,512]{0,1:T(8,128)(4,1)S(1)} %and_and_fusion.2, bf16[512,2,128,1]{0,2,3,1:T(8,128)(2,1)S(1)} %bitcast.72, bf16[256,2,8,128]{3,0,2,1:T(8,128)(2,1)S(1)} %get-tuple-element.448), kind=kOutput, calls=%fused_computation.5.clone.1 | convolution fusion | flops 543158272 | bytes 9846784 | tf_op jit(solution)/shard_map/while/body/eval_jaxpr/rgqd,ngd->gqrn/dot_general | solution.py:47
  363.9 4.6 fusion.33
  369.8 3.5 fusion.35
  376.9 5.3 %fusion.32 = (f32[2,8,256]{2,1,0:T(8,128)}, f32[2,512,256,8]{2,1,3,0:T(8,128)}) fusion(pred[256,512]{0,1:T(8,128)(4,1)S(1)} %and_and_fusion.2, bf16[512,2,128,1]{0,2,3,1:T(8,128)(2,1)S(1)} %bitcast.72, bf16[256,2,8,128]{3,0,2,1:T(8,128)(2,1)S(1)} %get-tuple-element.448), kind=kOutput, calls=%fused_computation.5.clone.1 | convolution fusion | flops 543158272 | bytes 9846784 | tf_op jit(solution)/shard_map/while/body/eval_jaxpr/rgqd,ngd->gqrn/dot_general | solution.py:47
  383.0 4.6 fusion.33
  388.8 3.5 fusion.35
  395.9 5.3 %fusion.32 = (f32[2,8,256]{2,1,0:T(8,128)}, f32[2,512,256,8]{2,1,3,0:T(8,128)}) fusion(pred[256,512]{0,1:T(8,128)(4,1)S(1)} %and_and_fusion.2, bf16[512,2,128,1]{0,2,3,1:T(8,128)(2,1)S(1)} %bitcast.72, bf16[256,2,8,128]{3,0,2,1:T(8,128)(2,1)S(1)} %get-tuple-element.448), kind=kOutput, calls=%fused_computation.5.clone.1 | convolution fusion | flops 543158272 | bytes 9846784 | tf_op jit(solution)/shard_map/while/body/eval_jaxpr/rgqd,ngd->gqrn/dot_general | solution.py:47
  402.0 4.6 fusion.33
  407.9 3.5 fusion.35
  415.0 5.3 %fusion.32 = (f32[2,8,256]{2,1,0:T(8,128)}, f32[2,512,256,8]{2,1,3,0:T(8,128)}) fusion(pred[256,512]{0,1:T(8,128)(4,1)S(1)} %and_and_fusion.2, bf16[512,2,128,1]{0,2,3,1:T(8,128)(2,1)S(1)} %bitcast.72, bf16[256,2,8,128]{3,0,2,1:T(8,128)(2,1)S(1)} %get-tuple-element.448), kind=kOutput, calls=%fused_computation.5.clone.1 | convolution fusion | flops 543158272 | bytes 9846784 | tf_op jit(solution)/shard_map/while/body/eval_jaxpr/rgqd,ngd->gqrn/dot_general | solution.py:47
  421.0 4.6 fusion.33
  426.9 3.5 fusion.35
  430.4 1.4 fusion.15
  433.1 22.4 %all_to_all.29 = bf16[32,8,2048]{2,1,0:T(8,128)(2,1)S(1)} all-to-all(bf16[32,8,2048]{2,1,0:T(8,128)(2,1)S(1)} %convert_element_type.56), channel_id=1, replica_groups=mesh['tok'=32,'kv'=4] {'tok'}, dimensions={0} | all-to-all | bytes 2097152 | tf_op jit(solution)/shard_map/all_to_all | solution.py:146
  456.5 4.6 scatter_fusion
  461.1 4.1 all-to-all-start.2
  465.9 13.9 %all-to-all-done.2 = bf16[4,64,2048]{2,1,0:T(8,128)(2,1)S(1)} async-done(((bf16[4,64,2048]{2,1,0:T(8,128)(2,1)}), bf16[4,64,2048]{2,1,0:T(8,128)(2,1)S(1)}, u32[]{:S(2)}, u32[]{:S(2)}) %all-to-all-start.2) | async-done | bytes 1048608 | tf_op jit(solution)/shard_map/all_to_all | solution.py:156
  (297 shorter events, 99.8 us)
Async XLA Ops:
  7.2 9.2 %copy-start.1 = (bf16[256,2048]{1,0:T(8,128)(2,1)S(1)}, bf16[256,2048]{1,0:T(8,128)(2,1)}, u32[]{:S(2)}) copy-start(bf16[256,2048]{1,0:T(8,128)(2,1)} %param.7) | copy-start | bytes 3145732
  7.2 67.7 %all-gather.3.cloned.1.call-start = ((), (), s32[]{:S(2)}) async-start(), calls=%async_computation.3 | async-start | bytes 4325376 | tf_op jit(solution)/shard_map/all_gather | solution.py:140
  14.4 111.4 %all-gather.5.cloned.1.call-start = ((), (), s32[]{:S(2)}) async-start(), calls=%async_computation.4 | async-start | bytes 4325376 | tf_op jit(solution)/shard_map/all_gather | solution.py:141
  19.5 0.5 copy-start.5
  22.5 27.0 %all-to-all-start = ((bf16[32,8,2048]{2,1,0:T(8,128)(2,1)}), bf16[32,8,2048]{2,1,0:T(8,128)(2,1)S(1)}, u32[]{:S(2)}, u32[]{:S(2)}) async-start(bf16[32,8,2048]{2,1,0:T(8,128)(2,1)} %broadcast_select_fusion), calls=%async_computation | async-start | bytes 2097152 | tf_op jit(solution)/shard_map/all_to_all | solution.py:122
  135.4 4.6 copy-start.2
  135.4 5.9 %copy-start = (f32[2,512,256,8]{2,1,3,0:T(8,128)S(1)}, f32[2,512,256,8]{2,1,3,0:T(8,128)}, u32[]{:S(2)}) copy-start(f32[2,512,256,8]{2,1,3,0:T(8,128)} %get-tuple-element.409) | copy-start | bytes 25165828 | tf_op jit(solution)/shard_map/while
  140.1 4.7 copy-start.3
  154.5 4.6 copy-start.2
  154.5 5.9 %copy-start = (f32[2,512,256,8]{2,1,3,0:T(8,128)S(1)}, f32[2,512,256,8]{2,1,3,0:T(8,128)}, u32[]{:S(2)}) copy-start(f32[2,512,256,8]{2,1,3,0:T(8,128)} %get-tuple-element.409) | copy-start | bytes 25165828 | tf_op jit(solution)/shard_map/while
  159.1 4.7 copy-start.3
  173.5 4.6 copy-start.2
  173.5 5.9 %copy-start = (f32[2,512,256,8]{2,1,3,0:T(8,128)S(1)}, f32[2,512,256,8]{2,1,3,0:T(8,128)}, u32[]{:S(2)}) copy-start(f32[2,512,256,8]{2,1,3,0:T(8,128)} %get-tuple-element.409) | copy-start | bytes 25165828 | tf_op jit(solution)/shard_map/while
  178.2 4.7 copy-start.3
  192.6 4.6 copy-start.2
  192.6 5.9 %copy-start = (f32[2,512,256,8]{2,1,3,0:T(8,128)S(1)}, f32[2,512,256,8]{2,1,3,0:T(8,128)}, u32[]{:S(2)}) copy-start(f32[2,512,256,8]{2,1,3,0:T(8,128)} %get-tuple-element.409) | copy-start | bytes 25165828 | tf_op jit(solution)/shard_map/while
  197.2 4.7 copy-start.3
  211.6 4.6 copy-start.2
  211.6 5.9 %copy-start = (f32[2,512,256,8]{2,1,3,0:T(8,128)S(1)}, f32[2,512,256,8]{2,1,3,0:T(8,128)}, u32[]{:S(2)}) copy-start(f32[2,512,256,8]{2,1,3,0:T(8,128)} %get-tuple-element.409) | copy-start | bytes 25165828 | tf_op jit(solution)/shard_map/while
  216.2 4.7 copy-start.3
  230.6 4.6 copy-start.2
  230.6 5.9 %copy-start = (f32[2,512,256,8]{2,1,3,0:T(8,128)S(1)}, f32[2,512,256,8]{2,1,3,0:T(8,128)}, u32[]{:S(2)}) copy-start(f32[2,512,256,8]{2,1,3,0:T(8,128)} %get-tuple-element.409) | copy-start | bytes 25165828 | tf_op jit(solution)/shard_map/while
  235.3 4.7 copy-start.3
  249.7 4.6 copy-start.2
  249.7 5.9 %copy-start = (f32[2,512,256,8]{2,1,3,0:T(8,128)S(1)}, f32[2,512,256,8]{2,1,3,0:T(8,128)}, u32[]{:S(2)}) copy-start(f32[2,512,256,8]{2,1,3,0:T(8,128)} %get-tuple-element.409) | copy-start | bytes 25165828 | tf_op jit(solution)/shard_map/while
  254.3 4.7 copy-start.3
  268.7 4.6 copy-start.2
  268.7 5.9 %copy-start = (f32[2,512,256,8]{2,1,3,0:T(8,128)S(1)}, f32[2,512,256,8]{2,1,3,0:T(8,128)}, u32[]{:S(2)}) copy-start(f32[2,512,256,8]{2,1,3,0:T(8,128)} %get-tuple-element.409) | copy-start | bytes 25165828 | tf_op jit(solution)/shard_map/while
  273.4 4.7 copy-start.3
  287.8 4.6 copy-start.2
  287.8 5.9 %copy-start = (f32[2,512,256,8]{2,1,3,0:T(8,128)S(1)}, f32[2,512,256,8]{2,1,3,0:T(8,128)}, u32[]{:S(2)}) copy-start(f32[2,512,256,8]{2,1,3,0:T(8,128)} %get-tuple-element.409) | copy-start | bytes 25165828 | tf_op jit(solution)/shard_map/while
  292.4 4.7 copy-start.3
  306.8 4.6 copy-start.2
  306.8 5.9 %copy-start = (f32[2,512,256,8]{2,1,3,0:T(8,128)S(1)}, f32[2,512,256,8]{2,1,3,0:T(8,128)}, u32[]{:S(2)}) copy-start(f32[2,512,256,8]{2,1,3,0:T(8,128)} %get-tuple-element.409) | copy-start | bytes 25165828 | tf_op jit(solution)/shard_map/while
  311.4 4.7 copy-start.3
  325.8 4.6 copy-start.2
  325.8 5.9 %copy-start = (f32[2,512,256,8]{2,1,3,0:T(8,128)S(1)}, f32[2,512,256,8]{2,1,3,0:T(8,128)}, u32[]{:S(2)}) copy-start(f32[2,512,256,8]{2,1,3,0:T(8,128)} %get-tuple-element.409) | copy-start | bytes 25165828 | tf_op jit(solution)/shard_map/while
  330.5 4.7 copy-start.3
  344.9 4.6 copy-start.2
  344.9 5.9 %copy-start = (f32[2,512,256,8]{2,1,3,0:T(8,128)S(1)}, f32[2,512,256,8]{2,1,3,0:T(8,128)}, u32[]{:S(2)}) copy-start(f32[2,512,256,8]{2,1,3,0:T(8,128)} %get-tuple-element.409) | copy-start | bytes 25165828 | tf_op jit(solution)/shard_map/while
  349.5 4.7 copy-start.3
  363.9 4.6 copy-start.2
  363.9 5.9 %copy-start = (f32[2,512,256,8]{2,1,3,0:T(8,128)S(1)}, f32[2,512,256,8]{2,1,3,0:T(8,128)}, u32[]{:S(2)}) copy-start(f32[2,512,256,8]{2,1,3,0:T(8,128)} %get-tuple-element.409) | copy-start | bytes 25165828 | tf_op jit(solution)/shard_map/while
  368.6 4.7 copy-start.3
  383.0 4.6 copy-start.2
  383.0 5.9 %copy-start = (f32[2,512,256,8]{2,1,3,0:T(8,128)S(1)}, f32[2,512,256,8]{2,1,3,0:T(8,128)}, u32[]{:S(2)}) copy-start(f32[2,512,256,8]{2,1,3,0:T(8,128)} %get-tuple-element.409) | copy-start | bytes 25165828 | tf_op jit(solution)/shard_map/while
  387.6 4.7 copy-start.3
  402.0 4.6 copy-start.2
  402.0 5.9 %copy-start = (f32[2,512,256,8]{2,1,3,0:T(8,128)S(1)}, f32[2,512,256,8]{2,1,3,0:T(8,128)}, u32[]{:S(2)}) copy-start(f32[2,512,256,8]{2,1,3,0:T(8,128)} %get-tuple-element.409) | copy-start | bytes 25165828 | tf_op jit(solution)/shard_map/while
  406.6 4.7 copy-start.3
  421.0 4.6 copy-start.2
  421.0 5.9 %copy-start = (f32[2,512,256,8]{2,1,3,0:T(8,128)S(1)}, f32[2,512,256,8]{2,1,3,0:T(8,128)}, u32[]{:S(2)}) copy-start(f32[2,512,256,8]{2,1,3,0:T(8,128)} %get-tuple-element.409) | copy-start | bytes 25165828 | tf_op jit(solution)/shard_map/while
  425.7 4.7 copy-start.3
  433.0 23.5 %copy-start.6 = (s32[32]{0:T(128)S(1)}, s32[32]{0:T(128)}, u32[]{:S(2)}) copy-start(s32[32]{0:T(128)} %copy-done.5) | copy-start | bytes 388
  456.5 8.7 %copy-start.4 = (f32[2,8,256]{2,1,0:T(8,128)S(1)}, f32[2,8,256]{2,1,0:T(8,128)}, u32[]{:S(2)}) copy-start(f32[2,8,256]{2,1,0:T(8,128)} %get-tuple-element.238) | copy-start | bytes 49156
  461.1 18.6 %all-to-all-start.2 = ((bf16[4,64,2048]{2,1,0:T(8,128)(2,1)}), bf16[4,64,2048]{2,1,0:T(8,128)(2,1)S(1)}, u32[]{:S(2)}, u32[]{:S(2)}) async-start(bf16[4,64,2048]{2,1,0:T(8,128)(2,1)} %bitcast.7), calls=%async_computation.2 | async-start | bytes 2097152 | tf_op jit(solution)/shard_map/all_to_all | solution.py:156
Sparse Core Ops, SparseCore 0:
  14.5 60.3 all-gather.2
  77.1 48.6 all-gather.4
where the time goes:
time: 490 us; the launch traced here: 488 us
  matrix products  141 us (29%)
  other arithmetic  136 us (28%)
  waiting for transfers between devices  108 us (22%)
  local copies, waits for them, and re-layouts  51.6 us (11%)
  blocking collectives  22.4 us (5%)
  between operations  14.3 us (3%)
  starting transfers between devices  12.8 us (3%)
    dot_general x16, matrix products, attend_block(): jnp.einsum('rgqd,ngd->gqrn', query_rows, key_rows, preferred_element_type...  85.4 us
    reduce_sum x16, other arithmetic, attend_block(): row_sum = row_sum * factor + jnp.sum(weights, axis=-1)  73.4 us
    dot_general x16, matrix products, attend_block(): jnp.einsum('gqrn,ngd->gqrd', probs, value_rows, preferred_element_type=jn...  55.7 us
    all_gather x1, waiting for transfers between devices, body(): lax.all_gather(value_states, 'tok', axis=0, tiled=True)  50.9 us
    all_gather x1, waiting for transfers between devices, body(): lax.all_gather(k_rot, 'tok', axis=0, tiled=True)  24.9 us
    all_to_all x1, blocking collectives, body(): lax.all_to_all(result.reshape(shards, block_rows, q_local * HEAD_DIM), 't...  22.4 us
    while x112, local copies, waits for them, and re-layouts  19.7 us
    all_to_all x1, waiting for transfers between devices, body(): lax.all_to_all(outgoing, 'tok', split_axis=0, concat_axis=0, tiled=True)  18.3 us
  transfers between devices with their start and end apart: 4, of which 4 were waited for; matrix products, arithmetic and copies ran while one was open for 2% of the time, Pallas kernels for 0%

commit v1 on v0

v1 whole, which is shorter than its diff:
```python
import functools
import math

import jax
import jax.numpy as jnp
import numpy as np
from jax import lax
from jax.experimental import pallas as pl
from jax.experimental.pallas import tpu as pltpu
from jax.sharding import PartitionSpec as P

D = 128
T = 256
GROUPS = 2
PER = 8
N_TOK = 32
N_KV = 4
DOCS = 16
BACK = 16
SLOTS = 24
NEG = -1e30
THETA = 500000.0
SCALE = 1.0 / math.sqrt(D)
C2 = SCALE * math.log2(math.e)
MESH = pl.DeviceIdType.MESH
BF = jnp.bfloat16
F32 = jnp.float32


def kernel(
    doc_ref, freq_ref, plan_ref, q_ref, k_ref, v_ref,
    out_ref, lse_ref,
    kv, qrot, scores, peak, obuf, start_ref, cos_ref, sin_ref, lse_own, lse_send, lse_recv,
    ksend, krecv, osend, orecv, lsend, lrecv,
):
    j = lax.axis_index("tok")
    z = lax.axis_index("kv")
    core = j % 2
    x = (j // 2) % 4
    y = j // 8
    pos = j % 8

    def tok_of(y_, x_, core_):
        return ((y_ % 4) * 4 + (x_ % 4)) * 2 + core_

    up = tok_of(y + 1, x, core)
    right = tok_of(y, x + 1, core)
    left = tok_of(y, x + 3, core)
    twin = tok_of(y, x, 1 - core)
    pos_r = (pos + 2) % 8
    pos_l = (pos + 6) % 8
    pos_f = (pos + 4) % 8

    barrier = pltpu.get_barrier_semaphore()

    def greet(d, _):
        pl.semaphore_signal(
            barrier, inc=1, device_id={"tok": (j + d) % N_TOK}, device_id_type=MESH
        )
        return 0

    lax.fori_loop(1, N_TOK, greet, 0)
    for d in range(1, N_KV):
        pl.semaphore_signal(
            barrier, inc=1, device_id={"kv": (z + d) % N_KV}, device_id_type=MESH
        )

    token = j * T + lax.broadcasted_iota(jnp.int32, (T, D), 0)
    lane = lax.broadcasted_iota(jnp.int32, (T, D), 1)
    start = jnp.zeros((T, D), jnp.int32)
    end = jnp.int32(0)
    for i in range(DOCS):
        end = end + doc_ref[i]
        start = jnp.where(token >= end, end, start)
    start_ref[...] = start - (j - BACK) * T
    angle = (token - start).astype(F32) * freq_ref[...]
    cos_ref[...] = jnp.cos(angle)
    sine = jnp.sin(angle)
    sin_ref[...] = jnp.where(lane < D // 2, -sine, sine)

    def rotate(block):
        wide = block.astype(F32)
        return (wide * cos_ref[...] + pltpu.roll(wide, D // 2, 1) * sin_ref[...]).astype(BF)

    for g in range(GROUPS):
        kv[2 * g, 16 + pos] = rotate(k_ref[:, g * D : (g + 1) * D])
        kv[2 * g + 1, 16 + pos] = v_ref[:, g * D : (g + 1) * D]

    pl.semaphore_wait(barrier, N_TOK - 1 + N_KV - 1)

    def copy(t, slot, n, to):
        return pltpu.make_async_remote_copy(
            src_ref=kv.at[t, slot],
            dst_ref=kv.at[t, slot],
            send_sem=ksend.at[t, n],
            recv_sem=krecv.at[t, slot],
            device_id={"tok": to},
            device_id_type=MESH,
        )

    def copy_up(t, row, n):
        return pltpu.make_async_remote_copy(
            src_ref=kv.at[t, row * 8 + pos],
            dst_ref=kv.at[t, (row - 1) * 8 + pos],
            send_sem=ksend.at[t, n],
            recv_sem=krecv.at[t, (row - 1) * 8 + pos],
            device_id={"tok": up},
            device_id_type=MESH,
        )

    def spread(t, row):
        n = row * 7
        copy(t, row * 8 + pos, n, right).start()
        copy(t, row * 8 + pos, n + 1, left).start()
        copy(t, row * 8 + pos, n + 2, twin).start()

    def pass_on(t, row):
        n = row * 7
        copy(t, row * 8 + pos_l, n + 3, right).wait_recv()
        copy(t, row * 8 + pos_r, n + 3, right).wait_recv()
        far_from = jnp.where(t % 2 == 0, pos_l, pos_r)
        far_to = jnp.where(t % 2 == 0, right, left)
        copy(t, row * 8 + far_from, n + 3, far_to).start()
        copy(t, row * 8 + pos_l, n + 4, twin).start()
        copy(t, row * 8 + pos_r, n + 5, twin).start()

    def last_on(t, row):
        copy(t, row * 8 + pos_f, row * 7 + 6, twin).wait_recv()
        copy(t, row * 8 + pos_f, row * 7 + 6, twin).start()

    def gather(t, _):
        copy_up(t, 2, 21).start()
        spread(t, 2)
        copy(t, 8 + pos, 0, up).wait_recv()
        copy_up(t, 1, 22).start()
        spread(t, 1)
        pass_on(t, 2)
        copy(t, pos, 0, up).wait_recv()
        spread(t, 0)
        pass_on(t, 1)
        last_on(t, 2)
        pass_on(t, 0)
        last_on(t, 1)
        last_on(t, 0)
        return 0

    def settle(t, _):
        def one(i, _):
            slot = (i // 4) * 8 + (i % 4) * 2 + 1 - core
            copy(t, slot, 0, twin).wait_recv()
            return 0

        lax.fori_loop(0, 12, one, 0)
        return 0

    def drain(t, _):
        def one(n, _):
            copy(t, 0, n, twin).wait_send()
            return 0

        lax.fori_loop(0, 23, one, 0)
        return 0

    for h in range(GROUPS * PER):
        qrot[h] = rotate(q_ref[:, h * D : (h + 1) * D])

    lax.fori_loop(0, 4, gather, 0)
    lax.fori_loop(0, 4, settle, 0)

    column = lax.broadcasted_iota(jnp.int32, (8, D), 1)

    def score(g, h, keys):
        return lax.dot_general(
            qrot[g * PER + h], keys, (((1,), (1,)), ((), ())), preferred_element_type=F32
        )

    def pass1(g):
        def pair(i, first):
            keys = jnp.concatenate([kv[2 * g, pos + 2 * i], kv[2 * g, pos + 2 * i + 1]], axis=0)

            def head(h, _):
                s = score(g, h, keys)
                best = peak[h]
                for c in range(4):
                    index = column + (i * 512 + c * D)
                    allowed = index[None] >= start_ref[...].reshape(T // 8, 8, D)
                    part = jnp.where(allowed.reshape(T, D), s[:, c * D : (c + 1) * D], NEG)
                    scores[i * 2 + c // 2, h, :, (c % 2) * D : (c % 2 + 1) * D] = part
                    best = jnp.maximum(best, part)
                peak[h] = best
                return 0

            lax.fori_loop(0, PER, head, 0, unroll=True)
            return first

        keys = kv[2 * g, pos + BACK]

        def diagonal(h, _):
            s = score(g, h, keys)
            row = lax.broadcasted_iota(jnp.int32, (T, D), 0)
            best = jnp.full((T, D), NEG, F32)
            for c in range(2):
                index = lax.broadcasted_iota(jnp.int32, (T, D), 1) + c * D
                allowed = (index + BACK * T >= start_ref[...]) & (index <= row)
                part = jnp.where(allowed, s[:, c * D : (c + 1) * D], NEG)
                scores[BACK, h, :, c * D : (c + 1) * D] = part
                best = jnp.maximum(best, part)
            peak[h] = best
            return 0

        lax.fori_loop(0, PER, diagonal, 0, unroll=True)
        lax.fori_loop(0, BACK // 2, pair, 0)

    def out_copy(head, d):
        to = (z + d) % N_KV
        return pltpu.make_async_remote_copy(
            src_ref=obuf.at[head, pl.ds(to * 64, 64), :],
            dst_ref=out_ref.at[:, pl.ds(pl.multiple_of((z * 16 + head) * D, D), D)],
            send_sem=osend.at[head, d],
            recv_sem=orecv.at[head, d],
            device_id={"kv": to},
            device_id_type=MESH,
        )

    def pass2(g):
        values = jnp.concatenate([kv[2 * g + 1, pos + i] for i in range(BACK + 1)], axis=0)

        def head(h, _):
            top = jnp.max(peak[h], axis=1, keepdims=True)
            wide = jnp.broadcast_to(top, (T, D))
            total = jnp.zeros((T, D), F32)
            probs = []
            for i in range(BACK + 1):
                for c in range(2):
                    p = jnp.exp2((scores[i, h, :, c * D : (c + 1) * D] - wide) * C2)
                    total = total + p
                    probs.append(p.astype(BF))
            mixed = jnp.dot(
                jnp.concatenate(probs, axis=1), values, preferred_element_type=F32
            )
            row_sum = jnp.sum(total, axis=1, keepdims=True)
            here = g * PER + h
            obuf[here] = (mixed / row_sum).astype(BF)
            norm = top * SCALE + jnp.log(row_sum)
            lse_own[...] = jnp.where(lane == here, norm, lse_own[...])
            for d in range(1, N_KV):
                out_copy(here, d).start()
            out_ref[:, pl.ds(pl.multiple_of((z * 16 + here) * D, D), D)] = obuf[
                here, pl.ds(pl.multiple_of(z * 64, 64), 64), :
            ]
            return 0

        lax.fori_loop(0, PER, head, 0)

    lse_own[...] = jnp.zeros((T, D), F32)
    for g in range(GROUPS):
        pass1(g)
        pass2(g)

    spread_rows = (
        lax.broadcasted_iota(jnp.int32, (T, N_TOK), 0) // 8
        == lax.broadcasted_iota(jnp.int32, (T, N_TOK), 1)
    ).astype(F32)
    plans = lax.dot_general(
        spread_rows.astype(BF), plan_ref[...].astype(F32).astype(BF),
        (((1,), (1,)), ((), ())), preferred_element_type=F32,
    )
    mine = lax.broadcasted_iota(jnp.int32, (T, N_TOK), 1) == j
    block = jnp.sum(jnp.where(mine, plans, 0.0), axis=1, keepdims=True).astype(jnp.int32)
    wanted = block * 8 + lax.broadcasted_iota(jnp.int32, (T, T), 0) % 8
    pick = (wanted == lax.broadcasted_iota(jnp.int32, (T, T), 1)).astype(F32).astype(BF)
    rest = lse_own[...]
    ordered = jnp.zeros((T, D), F32)
    for _ in range(3):
        piece = rest.astype(BF)
        rest = rest - piece.astype(F32)
        ordered = ordered + jnp.dot(pick, piece, preferred_element_type=F32)
    lse_send[...] = ordered.reshape(N_TOK, 8, D)
    lse_recv[j] = lse_send[j]

    def lse_copy(d):
        to = (j + d) % N_TOK
        return pltpu.make_async_remote_copy(
            src_ref=lse_send.at[to],
            dst_ref=lse_recv.at[j],
            send_sem=lsend.at[d],
            recv_sem=lrecv.at[d],
            device_id={"tok": to},
            device_id_type=MESH,
        )

    def lse_start(d, _):
        lse_copy(d).start()
        return 0

    def lse_wait(d, _):
        lse_copy(d).wait()
        return 0

    lax.fori_loop(1, N_TOK, lse_start, 0)
    lax.fori_loop(0, 4, drain, 0)
    lax.fori_loop(1, N_TOK, lse_wait, 0)
    lse_ref[...] = lse_recv[...].reshape(T, D).T[:16, :]

    def out_wait(h, _):
        for d in range(1, N_KV):
            out_copy(h, d).wait()
        return 0

    lax.fori_loop(0, GROUPS * PER, out_wait, 0)


def body(queries, key_states, value_states, doc_lengths, block_plan):
    half = np.power(THETA, -(np.arange(D // 2) * 2.0 / D)).astype(np.float32)
    freq = jnp.asarray(np.concatenate([half, half])[None, :])
    vmem = pl.BlockSpec(memory_space=pltpu.VMEM)
    return pl.pallas_call(
        kernel,
        out_shape=(
            jax.ShapeDtypeStruct((T // N_KV, N_KV * GROUPS * PER * D), BF),
            jax.ShapeDtypeStruct((GROUPS * PER, T), F32),
        ),
        in_specs=[pl.BlockSpec(memory_space=pltpu.SMEM)] + [vmem] * 5,
        out_specs=(vmem, vmem),
        scratch_shapes=[
            pltpu.VMEM((4, SLOTS, T, D), BF),
            pltpu.VMEM((GROUPS * PER, T, D), BF),
            pltpu.VMEM((BACK + 1, PER, T, T), F32),
            pltpu.VMEM((PER, T, D), F32),
            pltpu.VMEM((GROUPS * PER, T, D), BF),
            pltpu.VMEM((T, D), jnp.int32),
            pltpu.VMEM((T, D), F32),
            pltpu.VMEM((T, D), F32),
            pltpu.VMEM((T, D), F32),
            pltpu.VMEM((N_TOK, 8, D), F32),
            pltpu.VMEM((N_TOK, 8, D), F32),
            pltpu.SemaphoreType.DMA((4, 23)),
            pltpu.SemaphoreType.DMA((4, SLOTS)),
            pltpu.SemaphoreType.DMA((GROUPS * PER, N_KV)),
            pltpu.SemaphoreType.DMA((GROUPS * PER, N_KV)),
            pltpu.SemaphoreType.DMA((N_TOK,)),
            pltpu.SemaphoreType.DMA((N_TOK,)),
        ],
        compiler_params=pltpu.CompilerParams(
            collective_id=0, has_side_effects=True, vmem_limit_bytes=60 << 20
        ),
    )(doc_lengths, freq, block_plan, queries, key_states, value_states)


def solution(mesh):
    return jax.shard_map(
        body,
        mesh=mesh,
        in_specs=(P("tok", "kv"), P("tok", "kv"), P("tok", "kv"), P(), P()),
        out_specs=(P(("tok", "kv"), None), P("kv", "tok")),
        check_vma=False,
    )
```

time: 490 us -> 117 us (0.24)
  matrix products: 141 us -> 0 us
  other arithmetic: 136 us -> 0 us
  Pallas kernels: 0 us -> 113 us
  waiting for transfers between devices: 108 us -> 0 us
  local copies, waits for them, and re-layouts: 51.6 us -> 2.88 us
  blocking collectives: 22.4 us -> 0 us
  between operations: 14.3 us -> 0.65 us
  starting transfers between devices: 12.8 us -> 0 us
    dot_general x32 -> x0, matrix products: 141 us -> none  [the longest x16 85.4 us: attend_block(): jnp.einsum('rgqd,ngd->gqrn', query_rows, key_rows, preferred_element_type...]
    pallas_call x0 -> x1, Pallas kernels: none -> 113 us  [body(): pl.pallas_call(kernel, out_shape=(jax.ShapeDtypeStruct((T // N_KV, N_KV *...]
    reduce_sum x33 -> x0, other arithmetic: 86.2 us -> none  [the longest x16 73.4 us: attend_block(): row_sum = row_sum * factor + jnp.sum(weights, axis=-1)]
    all_gather x2 -> x0, waiting for transfers between devices: 75.8 us -> none  [the longest x1 50.9 us: body(): lax.all_gather(value_states, 'tok', axis=0, tiled=True)]
    all_to_all x2 -> x0, waiting for transfers between devices: 32.2 us -> none  [the longest x1 18.3 us: body(): lax.all_to_all(outgoing, 'tok', split_axis=0, concat_axis=0, tiled=True)]
    all_to_all x1 -> x0, blocking collectives: 22.4 us -> none  [body(): lax.all_to_all(result.reshape(shards, block_rows, q_local * HEAD_DIM), 't...]
    while x112 -> x0, local copies, waits for them, and re-layouts: 19.7 us -> none
    dynamic_slice x16 -> x0, local copies, waits for them, and re-layouts: 17.1 us -> none  [inner(): lax.dynamic_slice_in_dim(value_piece, offset, stride, 0)]
  transfers between devices with their start and end apart: 4 -> 0, of which waited for: 4 -> 0; matrix products, arithmetic and copies ran while one was open for 2% -> 0% of each run, Pallas kernels for 0% -> 0%
where the time goes in v1:
time: 117 us; the launch traced here: 116 us
  Pallas kernels  113 us (97%)
  local copies, waits for them, and re-layouts  2.88 us (2%)
    pallas_call x1, Pallas kernels, body(): pl.pallas_call(kernel, out_shape=(jax.ShapeDtypeStruct((T // N_KV, N_KV *...  113 us
    unnamed x4, local copies, waits for them, and re-layouts  2.88 us

profile of v1, /device:TPU:1, one launch (start us, length us, event | category | flops | bytes accessed | tf_op | source)
XLA Modules:
  0.0 116.4 jit_solution(6294331337848130348)
XLA Ops:
  0.6 112.9 %shard_map.77 = (bf16[64,8192]{1,0:T(8,128)(2,1)}, f32[16,256]{1,0:T(8,128)}) custom-call(s32[16]{0:T(128)} %doc_ref.1, f32[1,128]{1,0:T(1,128)} %constant.2.clone.freq_ref, s32[32,32]{1,0:T(8,128)} %plan_ref.1, bf16[256,2048]{1,0:T(8,128)(2,1)} %q_ref.1, bf16[256,256]{1,0:T(8,128)(2,1)} %k_ref.1, bf16[256,256]{1,0:T(8,128)(2,1)} %v_ref.1), custom_call_target="tpu_custom_call" | custom-call | tf_op jit(solution)/shard_map/pallas_call | solution.py:317
  113.5 0.0 copy-start
  113.5 2.3 %copy.10 = bf16[64,8192]{1,0:T(8,128)(2,1)} copy(bf16[64,8192]{1,0:T(8,128)(2,1)} %get-tuple-element.4) | data formatting | bytes 2097152
  115.8 0.0 copy-done
  115.8 0.6 copy.11
Async XLA Ops:
  113.5 2.3 %copy-start = (f32[16,256]{1,0:T(8,128)S(1)}, f32[16,256]{1,0:T(8,128)}, u32[]{:S(2)}) copy-start(f32[16,256]{1,0:T(8,128)} %get-tuple-element.5) | copy-start | bytes 49156

commit v2 on v1

--- a/solution.py
+++ b/solution.py
@@ -128,30 +128,25 @@
         copy(t, row * 8 + pos_f, row * 7 + 6, twin).wait_recv()
         copy(t, row * 8 + pos_f, row * 7 + 6, twin).start()
 
-    def gather(t, _):
+    def stage_a(t):
         copy_up(t, 2, 21).start()
         spread(t, 2)
+
+    def stage_b(t):
         copy(t, 8 + pos, 0, up).wait_recv()
         copy_up(t, 1, 22).start()
         spread(t, 1)
-        pass_on(t, 2)
+
+    def stage_d(t):
         copy(t, pos, 0, up).wait_recv()
         spread(t, 0)
-        pass_on(t, 1)
-        last_on(t, 2)
-        pass_on(t, 0)
-        last_on(t, 1)
-        last_on(t, 0)
-        return 0
-
-    def settle(t, _):
+
+    def settle(t, row):
         def one(i, _):
-            slot = (i // 4) * 8 + (i % 4) * 2 + 1 - core
-            copy(t, slot, 0, twin).wait_recv()
+            copy(t, row * 8 + i * 2 + 1 - core, 0, twin).wait_recv()
             return 0
 
-        lax.fori_loop(0, 12, one, 0)
-        return 0
+        lax.fori_loop(0, 4, one, 0)
 
     def drain(t, _):
         def one(n, _):
@@ -161,11 +156,25 @@
         lax.fori_loop(0, 23, one, 0)
         return 0
 
-    for h in range(GROUPS * PER):
-        qrot[h] = rotate(q_ref[:, h * D : (h + 1) * D])
-
-    lax.fori_loop(0, 4, gather, 0)
-    lax.fori_loop(0, 4, settle, 0)
+    def turn(h, _):
+        lanes = pl.ds(pl.multiple_of(h * D, D), D)
+        qrot[h] = rotate(q_ref[:, lanes])
+        return 0
+
+    stage_a(0)
+    lax.fori_loop(0, PER, turn, 0)
+    stage_b(0)
+    pass_on(0, 2)
+    stage_d(0)
+    pass_on(0, 1)
+    last_on(0, 2)
+    stage_a(1)
+    lax.fori_loop(PER, 2 * PER, turn, 0)
+    last_on(0, 1)
+    pass_on(0, 0)
+    settle(0, 2)
+    settle(0, 1)
+    stage_b(1)
 
     column = lax.broadcasted_iota(jnp.int32, (8, D), 1)
 
@@ -174,8 +183,10 @@
             qrot[g * PER + h], keys, (((1,), (1,)), ((), ())), preferred_element_type=F32
         )
 
-    def pass1(g):
-        def pair(i, first):
+    def pass1(g, hooks):
+        def pair(k, _):
+            hooks(k)
+            i = BACK // 2 - 1 - k
             keys = jnp.concatenate([kv[2 * g, pos + 2 * i], kv[2 * g, pos + 2 * i + 1]], axis=0)
 
             def head(h, _):
@@ -191,7 +202,7 @@
                 return 0
 
             lax.fori_loop(0, PER, head, 0, unroll=True)
-            return first
+            return 0
 
         keys = kv[2 * g, pos + BACK]
 
@@ -222,10 +233,11 @@
             device_id_type=MESH,
         )
 
-    def pass2(g):
+    def pass2(g, hooks):
         values = jnp.concatenate([kv[2 * g + 1, pos + i] for i in range(BACK + 1)], axis=0)
 
         def head(h, _):
+            hooks(h)
             top = jnp.max(peak[h], axis=1, keepdims=True)
             wide = jnp.broadcast_to(top, (T, D))
             total = jnp.zeros((T, D), F32)
@@ -253,9 +265,46 @@
         lax.fori_loop(0, PER, head, 0)
 
     lse_own[...] = jnp.zeros((T, D), F32)
-    for g in range(GROUPS):
-        pass1(g)
-        pass2(g)
+    def hooks_of(table):
+        def hooks(k):
+            for step, calls in table.items():
+
+                @pl.when(k == step)
+                def _():
+                    for call, *where in calls:
+                        call(*where)
+
+        return hooks
+
+    pass1(0, hooks_of({
+        0: [(pass_on, 1, 2)],
+        1: [(last_on, 0, 0), (stage_d, 1)],
+        2: [(pass_on, 1, 1), (last_on, 1, 2)],
+        4: [(settle, 0, 0), (pass_on, 1, 0)],
+        5: [(last_on, 1, 1), (stage_a, 2)],
+        7: [(last_on, 1, 0), (stage_b, 2)],
+    }))
+    for row in range(3):
+        settle(1, row)
+    pass2(0, hooks_of({
+        0: [(pass_on, 2, 2), (stage_d, 2)],
+        2: [(pass_on, 2, 1), (last_on, 2, 2)],
+        3: [(stage_a, 3)],
+        4: [(pass_on, 2, 0), (last_on, 2, 1)],
+        5: [(stage_b, 3), (pass_on, 3, 2)],
+        6: [(last_on, 2, 0)],
+        7: [(stage_d, 3)],
+    }))
+    for row in range(3):
+        settle(2, row)
+    pass1(1, hooks_of({
+        0: [(pass_on, 3, 1), (last_on, 3, 2)],
+        2: [(pass_on, 3, 0), (last_on, 3, 1)],
+        4: [(last_on, 3, 0)],
+    }))
+    for row in range(3):
+        settle(3, row)
+    pass2(1, lambda h: None)
 
     spread_rows = (
         lax.broadcasted_iota(jnp.int32, (T, N_TOK), 0) // 8

time: 117 us -> 86.1 us (0.74)
  Pallas kernels: 113 us -> 82.5 us
    pallas_call x1, Pallas kernels: 113 us -> 82.5 us  [body(): pl.pallas_call(kernel, out_shape=(jax.ShapeDtypeStruct((T // N_KV, N_KV *...]
where the time goes in v2:
time: 86.1 us; the launch traced here: 86 us
  Pallas kernels  82.5 us (96%)
  local copies, waits for them, and re-layouts  2.88 us (3%)
    pallas_call x1, Pallas kernels, body(): pl.pallas_call(kernel, out_shape=(jax.ShapeDtypeStruct((T // N_KV, N_KV *...  82.5 us
    unnamed x4, local copies, waits for them, and re-layouts  2.88 us

profile of v2, /device:TPU:1, one launch (start us, length us, event | category | flops | bytes accessed | tf_op | source)
XLA Modules:
  0.0 86.0 jit_solution(18173665952307483217)
XLA Ops:
  0.6 82.5 %shard_map.77 = (bf16[64,8192]{1,0:T(8,128)(2,1)}, f32[16,256]{1,0:T(8,128)}) custom-call(s32[16]{0:T(128)} %doc_ref.1, f32[1,128]{1,0:T(1,128)} %constant.2.clone.freq_ref, s32[32,32]{1,0:T(8,128)} %plan_ref.1, bf16[256,2048]{1,0:T(8,128)(2,1)} %q_ref.1, bf16[256,256]{1,0:T(8,128)(2,1)} %k_ref.1, bf16[256,256]{1,0:T(8,128)(2,1)} %v_ref.1), custom_call_target="tpu_custom_call" | custom-call | tf_op jit(solution)/shard_map/pallas_call | solution.py:366
  83.1 0.0 copy-start
  83.1 2.3 %copy.10 = bf16[64,8192]{1,0:T(8,128)(2,1)} copy(bf16[64,8192]{1,0:T(8,128)(2,1)} %get-tuple-element.4) | data formatting | bytes 2097152
  85.4 0.0 copy-done
  85.4 0.6 copy.11
Async XLA Ops:
  83.1 2.3 %copy-start = (f32[16,256]{1,0:T(8,128)S(1)}, f32[16,256]{1,0:T(8,128)}, u32[]{:S(2)}) copy-start(f32[16,256]{1,0:T(8,128)} %get-tuple-element.5) | copy-start | bytes 49156

commit v3 on v2

--- a/solution.py
+++ b/solution.py
@@ -28,10 +28,10 @@
 
 
 def kernel(
-    doc_ref, freq_ref, plan_ref, q_ref, k_ref, v_ref,
+    doc_ref, freq_ref, plan_ref, q_hbm, k_hbm, v_hbm,
     out_ref, lse_ref,
-    kv, qrot, scores, peak, obuf, start_ref, cos_ref, sin_ref, lse_own, lse_send, lse_recv,
-    ksend, krecv, osend, orecv, lsend, lrecv,
+    q_ref, k_ref, v_ref, kv, qrot, scores, peak, obuf, start_ref, cos_ref, sin_ref, lse_own, lse_send, lse_recv,
+    insem, ksend, krecv, trecv, osend, orecv, lsend, lrecv,
 ):
     j = lax.axis_index("tok")
     z = lax.axis_index("kv")
@@ -39,17 +39,18 @@
     x = (j // 2) % 4
     y = j // 8
     pos = j % 8
+    own = core * 4 + x
+
+    loads = [
+        pltpu.make_async_copy(k_hbm, k_ref, insem.at[0]),
+        pltpu.make_async_copy(v_hbm, v_ref, insem.at[1]),
+        pltpu.make_async_copy(q_hbm, q_ref, insem.at[2]),
+    ]
+    for load in loads:
+        load.start()
 
     def tok_of(y_, x_, core_):
         return ((y_ % 4) * 4 + (x_ % 4)) * 2 + core_
-
-    up = tok_of(y + 1, x, core)
-    right = tok_of(y, x + 1, core)
-    left = tok_of(y, x + 3, core)
-    twin = tok_of(y, x, 1 - core)
-    pos_r = (pos + 2) % 8
-    pos_l = (pos + 6) % 8
-    pos_f = (pos + 4) % 8
 
     barrier = pltpu.get_barrier_semaphore()
 
@@ -82,79 +83,82 @@
         wide = block.astype(F32)
         return (wide * cos_ref[...] + pltpu.roll(wide, D // 2, 1) * sin_ref[...]).astype(BF)
 
+    loads[0].wait()
+    loads[1].wait()
     for g in range(GROUPS):
-        kv[2 * g, 16 + pos] = rotate(k_ref[:, g * D : (g + 1) * D])
-        kv[2 * g + 1, 16 + pos] = v_ref[:, g * D : (g + 1) * D]
+        kv[2 * g, 16 + own] = rotate(k_ref[:, g * D : (g + 1) * D])
+        kv[2 * g + 1, 16 + own] = v_ref[:, g * D : (g + 1) * D]
 
     pl.semaphore_wait(barrier, N_TOK - 1 + N_KV - 1)
 
-    def copy(t, slot, n, to):
+    def copy(t, source, target, to):
         return pltpu.make_async_remote_copy(
-            src_ref=kv.at[t, slot],
-            dst_ref=kv.at[t, slot],
-            send_sem=ksend.at[t, n],
-            recv_sem=krecv.at[t, slot],
+            src_ref=kv.at[t, source],
+            dst_ref=kv.at[t, target],
+            send_sem=ksend.at[t],
+            recv_sem=krecv.at[t, target],
             device_id={"tok": to},
             device_id_type=MESH,
         )
 
-    def copy_up(t, row, n):
+    def share(t, row):
+        mine = pl.ds(row * 8 + core * 4, 4)
         return pltpu.make_async_remote_copy(
-            src_ref=kv.at[t, row * 8 + pos],
-            dst_ref=kv.at[t, (row - 1) * 8 + pos],
-            send_sem=ksend.at[t, n],
-            recv_sem=krecv.at[t, (row - 1) * 8 + pos],
-            device_id={"tok": up},
+            src_ref=kv.at[t, mine],
+            dst_ref=kv.at[t, mine],
+            send_sem=ksend.at[t],
+            recv_sem=trecv.at[t, row],
+            device_id={"tok": tok_of(y, x, 1 - core)},
             device_id_type=MESH,
         )
 
+    def needs(row, source_x, target_x):
+        return (target_x > source_x) if row == 2 else (target_x < source_x)
+
     def spread(t, row):
-        n = row * 7
-        copy(t, row * 8 + pos, n, right).start()
-        copy(t, row * 8 + pos, n + 1, left).start()
-        copy(t, row * 8 + pos, n + 2, twin).start()
-
-    def pass_on(t, row):
-        n = row * 7
-        copy(t, row * 8 + pos_l, n + 3, right).wait_recv()
-        copy(t, row * 8 + pos_r, n + 3, right).wait_recv()
-        far_from = jnp.where(t % 2 == 0, pos_l, pos_r)
-        far_to = jnp.where(t % 2 == 0, right, left)
-        copy(t, row * 8 + far_from, n + 3, far_to).start()
-        copy(t, row * 8 + pos_l, n + 4, twin).start()
-        copy(t, row * 8 + pos_r, n + 5, twin).start()
-
-    def last_on(t, row):
-        copy(t, row * 8 + pos_f, row * 7 + 6, twin).wait_recv()
-        copy(t, row * 8 + pos_f, row * 7 + 6, twin).start()
+        slot = row * 8 + own
+        for d in (1, 3, 2):
+            target_x = (x + d) % 4
+
+            def send():
+                copy(t, slot, slot, tok_of(y, target_x, core)).start()
+
+            if row == 1:
+                send()
+            else:
+                pl.when(needs(row, x, target_x))(send)
 
     def stage_a(t):
-        copy_up(t, 2, 21).start()
+        for d in (1, 2):
+            copy(t, 16 + own, 16 - 8 * d + own, tok_of(y + d, x, core)).start()
         spread(t, 2)
 
     def stage_b(t):
-        copy(t, 8 + pos, 0, up).wait_recv()
-        copy_up(t, 1, 22).start()
-        spread(t, 1)
-
-    def stage_d(t):
-        copy(t, pos, 0, up).wait_recv()
-        spread(t, 0)
+        for row in (1, 0):
+            copy(t, 0, row * 8 + own, j).wait_recv()
+            spread(t, row)
+
+    def stage_t(t, row):
+        for d in (1, 3, 2):
+            source_x = (x + 4 - d) % 4
+
+            def arrive():
+                copy(t, 0, row * 8 + core * 4 + source_x, j).wait_recv()
+
+            if row == 1:
+                arrive()
+            else:
+                pl.when(needs(row, source_x, x))(arrive)
+        share(t, row).start()
 
     def settle(t, row):
-        def one(i, _):
-            copy(t, row * 8 + i * 2 + 1 - core, 0, twin).wait_recv()
-            return 0
-
-        lax.fori_loop(0, 4, one, 0)
-
-    def drain(t, _):
-        def one(n, _):
-            copy(t, 0, n, twin).wait_send()
-            return 0
-
-        lax.fori_loop(0, 23, one, 0)
-        return 0
+        pltpu.make_async_copy(
+            kv.at[t, pl.ds(0, 4)], kv.at[t, pl.ds(row * 8, 4)], trecv.at[t, row]
+        ).wait()
+
+    def drain(t):
+        part = kv.at[t, pl.ds(0, 20)]
+        pltpu.make_async_copy(part, part, ksend.at[t]).wait()
 
     def turn(h, _):
         lanes = pl.ds(pl.multiple_of(h * D, D), D)
@@ -162,19 +166,22 @@
         return 0
 
     stage_a(0)
+    loads[2].wait()
     lax.fori_loop(0, PER, turn, 0)
     stage_b(0)
-    pass_on(0, 2)
-    stage_d(0)
-    pass_on(0, 1)
-    last_on(0, 2)
     stage_a(1)
     lax.fori_loop(PER, 2 * PER, turn, 0)
-    last_on(0, 1)
-    pass_on(0, 0)
+    stage_t(0, 2)
+    stage_t(0, 1)
+    stage_b(1)
+    stage_t(0, 0)
     settle(0, 2)
     settle(0, 1)
-    stage_b(1)
+
+    def tile(t, i):
+        at = pos + i
+        place = at % 8
+        return kv[t, (at // 8) * 8 + (place % 2) * 4 + place // 2]
 
     column = lax.broadcasted_iota(jnp.int32, (8, D), 1)
 
@@ -187,7 +194,7 @@
         def pair(k, _):
             hooks(k)
             i = BACK // 2 - 1 - k
-            keys = jnp.concatenate([kv[2 * g, pos + 2 * i], kv[2 * g, pos + 2 * i + 1]], axis=0)
+            keys = jnp.concatenate([tile(2 * g, 2 * i), tile(2 * g, 2 * i + 1)], axis=0)
 
             def head(h, _):
                 s = score(g, h, keys)
@@ -204,7 +211,7 @@
             lax.fori_loop(0, PER, head, 0, unroll=True)
             return 0
 
-        keys = kv[2 * g, pos + BACK]
+        keys = tile(2 * g, BACK)
 
         def diagonal(h, _):
             s = score(g, h, keys)
@@ -227,14 +234,14 @@
         return pltpu.make_async_remote_copy(
             src_ref=obuf.at[head, pl.ds(to * 64, 64), :],
             dst_ref=out_ref.at[:, pl.ds(pl.multiple_of((z * 16 + head) * D, D), D)],
-            send_sem=osend.at[head, d],
-            recv_sem=orecv.at[head, d],
+            send_sem=osend.at[0],
+            recv_sem=orecv.at[0],
             device_id={"kv": to},
             device_id_type=MESH,
         )
 
     def pass2(g, hooks):
-        values = jnp.concatenate([kv[2 * g + 1, pos + i] for i in range(BACK + 1)], axis=0)
+        values = jnp.concatenate([tile(2 * g + 1, i) for i in range(BACK + 1)], axis=0)
 
         def head(h, _):
             hooks(h)
@@ -277,31 +284,24 @@
         return hooks
 
     pass1(0, hooks_of({
-        0: [(pass_on, 1, 2)],
-        1: [(last_on, 0, 0), (stage_d, 1)],
-        2: [(pass_on, 1, 1), (last_on, 1, 2)],
-        4: [(settle, 0, 0), (pass_on, 1, 0)],
-        5: [(last_on, 1, 1), (stage_a, 2)],
-        7: [(last_on, 1, 0), (stage_b, 2)],
+        0: [(stage_a, 2)],
+        1: [(stage_t, 1, 2), (stage_t, 1, 1)],
+        2: [(stage_t, 1, 0)],
+        4: [(settle, 0, 0), (stage_b, 2)],
+        6: [(stage_a, 3)],
     }))
     for row in range(3):
         settle(1, row)
     pass2(0, hooks_of({
-        0: [(pass_on, 2, 2), (stage_d, 2)],
-        2: [(pass_on, 2, 1), (last_on, 2, 2)],
-        3: [(stage_a, 3)],
-        4: [(pass_on, 2, 0), (last_on, 2, 1)],
-        5: [(stage_b, 3), (pass_on, 3, 2)],
-        6: [(last_on, 2, 0)],
-        7: [(stage_d, 3)],
+        0: [(stage_t, 2, 2), (stage_t, 2, 1)],
+        1: [(stage_t, 2, 0)],
+        2: [(stage_b, 3)],
+        5: [(stage_t, 3, 2), (stage_t, 3, 1)],
+        6: [(stage_t, 3, 0)],
     }))
     for row in range(3):
         settle(2, row)
-    pass1(1, hooks_of({
-        0: [(pass_on, 3, 1), (last_on, 3, 2)],
-        2: [(pass_on, 3, 0), (last_on, 3, 1)],
-        4: [(last_on, 3, 0)],
-    }))
+    pass1(1, lambda k: None)
     for row in range(3):
         settle(3, row)
     pass2(1, lambda h: None)
@@ -332,8 +332,8 @@
         return pltpu.make_async_remote_copy(
             src_ref=lse_send.at[to],
             dst_ref=lse_recv.at[j],
-            send_sem=lsend.at[d],
-            recv_sem=lrecv.at[d],
+            send_sem=lsend.at[0],
+            recv_sem=lrecv.at[0],
             device_id={"tok": to},
             device_id_type=MESH,
         )
@@ -342,36 +342,36 @@
         lse_copy(d).start()
         return 0
 
-    def lse_wait(d, _):
-        lse_copy(d).wait()
-        return 0
+    def finish(part, sem):
+        pltpu.make_async_copy(part, part, sem.at[0]).wait()
 
     lax.fori_loop(1, N_TOK, lse_start, 0)
-    lax.fori_loop(0, 4, drain, 0)
-    lax.fori_loop(1, N_TOK, lse_wait, 0)
+    for t in range(4):
+        drain(t)
+    finish(lse_recv.at[pl.ds(0, N_TOK - 1)], lrecv)
     lse_ref[...] = lse_recv[...].reshape(T, D).T[:16, :]
-
-    def out_wait(h, _):
-        for d in range(1, N_KV):
-            out_copy(h, d).wait()
-        return 0
-
-    lax.fori_loop(0, GROUPS * PER, out_wait, 0)
+    finish(lse_send.at[pl.ds(0, N_TOK - 1)], lsend)
+    finish(obuf.at[pl.ds(0, 12)], osend)
+    finish(out_ref.at[:, pl.ds(0, 48 * D)], orecv)
 
 
 def body(queries, key_states, value_states, doc_lengths, block_plan):
     half = np.power(THETA, -(np.arange(D // 2) * 2.0 / D)).astype(np.float32)
     freq = jnp.asarray(np.concatenate([half, half])[None, :])
     vmem = pl.BlockSpec(memory_space=pltpu.VMEM)
+    far = pl.BlockSpec(memory_space=pl.ANY)
     return pl.pallas_call(
         kernel,
         out_shape=(
             jax.ShapeDtypeStruct((T // N_KV, N_KV * GROUPS * PER * D), BF),
             jax.ShapeDtypeStruct((GROUPS * PER, T), F32),
         ),
-        in_specs=[pl.BlockSpec(memory_space=pltpu.SMEM)] + [vmem] * 5,
+        in_specs=[pl.BlockSpec(memory_space=pltpu.SMEM)] + [vmem] * 2 + [far] * 3,
         out_specs=(vmem, vmem),
         scratch_shapes=[
+            pltpu.VMEM((T, GROUPS * PER * D), BF),
+            pltpu.VMEM((T, GROUPS * D), BF),
+            pltpu.VMEM((T, GROUPS * D), BF),
             pltpu.VMEM((4, SLOTS, T, D), BF),
             pltpu.VMEM((GROUPS * PER, T, D), BF),
             pltpu.VMEM((BACK + 1, PER, T, T), F32),
@@ -383,12 +383,14 @@
             pltpu.VMEM((T, D), F32),
             pltpu.VMEM((N_TOK, 8, D), F32),
             pltpu.VMEM((N_TOK, 8, D), F32),
-            pltpu.SemaphoreType.DMA((4, 23)),
+            pltpu.SemaphoreType.DMA((3,)),
+            pltpu.SemaphoreType.DMA((4,)),
             pltpu.SemaphoreType.DMA((4, SLOTS)),
-            pltpu.SemaphoreType.DMA((GROUPS * PER, N_KV)),
-            pltpu.SemaphoreType.DMA((GROUPS * PER, N_KV)),
-            pltpu.SemaphoreType.DMA((N_TOK,)),
-            pltpu.SemaphoreType.DMA((N_TOK,)),
+            pltpu.SemaphoreType.DMA((4, 3)),
+            pltpu.SemaphoreType.DMA((1,)),
+            pltpu.SemaphoreType.DMA((1,)),
+            pltpu.SemaphoreType.DMA((1,)),
+            pltpu.SemaphoreType.DMA((1,)),
         ],
         compiler_params=pltpu.CompilerParams(
             collective_id=0, has_side_effects=True, vmem_limit_bytes=60 << 20

time: 86.1 us -> 71.7 us (0.83)
  Pallas kernels: 82.5 us -> 68 us
    pallas_call x1, Pallas kernels: 82.5 us -> 68 us  [body(): pl.pallas_call(kernel, out_shape=(jax.ShapeDtypeStruct((T // N_KV, N_KV *...]
where the time goes in v3:
time: 71.7 us; the launch traced here: 71.5 us
  Pallas kernels  68 us (95%)
  local copies, waits for them, and re-layouts  2.88 us (4%)
    pallas_call x1, Pallas kernels, body(): pl.pallas_call(kernel, out_shape=(jax.ShapeDtypeStruct((T // N_KV, N_KV *...  68 us
    unnamed x4, local copies, waits for them, and re-layouts  2.88 us

profile of v3, /device:TPU:1, one launch (start us, length us, event | category | flops | bytes accessed | tf_op | source)
XLA Modules:
  0.0 71.5 jit_solution(18044697248388080651)
XLA Ops:
  0.6 68.0 %shard_map.77 = (bf16[64,8192]{1,0:T(8,128)(2,1)}, f32[16,256]{1,0:T(8,128)}) custom-call(s32[16]{0:T(128)} %doc_ref.1, f32[1,128]{1,0:T(1,128)} %constant.2.clone.freq_ref, s32[32,32]{1,0:T(8,128)} %plan_ref.1, bf16[256,2048]{1,0:T(8,128)(2,1)} %q_hbm.1, bf16[256,256]{1,0:T(8,128)(2,1)} %k_hbm.1, bf16[256,256]{1,0:T(8,128)(2,1)} %v_hbm.1), custom_call_target="tpu_custom_call" | custom-call | tf_op jit(solution)/shard_map/pallas_call | solution.py:363
  68.6 0.0 copy-start
  68.6 2.3 %copy.10 = bf16[64,8192]{1,0:T(8,128)(2,1)} copy(bf16[64,8192]{1,0:T(8,128)(2,1)} %get-tuple-element.4) | data formatting | bytes 2097152
  70.9 0.0 copy-done
  70.9 0.6 copy.11
Async XLA Ops:
  68.6 2.3 %copy-start = (f32[16,256]{1,0:T(8,128)S(1)}, f32[16,256]{1,0:T(8,128)}, u32[]{:S(2)}) copy-start(f32[16,256]{1,0:T(8,128)} %get-tuple-element.5) | copy-start | bytes 49156

commit v4 on v3

--- a/solution.py
+++ b/solution.py
@@ -190,20 +190,19 @@
             qrot[g * PER + h], keys, (((1,), (1,)), ((), ())), preferred_element_type=F32
         )
 
-    def pass1(g, hooks):
+    def pass1(g, lo, hi):
         def pair(k, _):
-            hooks(k)
-            i = BACK // 2 - 1 - k
-            keys = jnp.concatenate([tile(2 * g, 2 * i), tile(2 * g, 2 * i + 1)], axis=0)
+            i = BACK // 4 - 1 - k
+            keys = jnp.concatenate([tile(2 * g, 4 * i + e) for e in range(4)], axis=0)
 
             def head(h, _):
                 s = score(g, h, keys)
                 best = peak[h]
-                for c in range(4):
-                    index = column + (i * 512 + c * D)
+                for c in range(8):
+                    index = column + (i * 1024 + c * D)
                     allowed = index[None] >= start_ref[...].reshape(T // 8, 8, D)
                     part = jnp.where(allowed.reshape(T, D), s[:, c * D : (c + 1) * D], NEG)
-                    scores[i * 2 + c // 2, h, :, (c % 2) * D : (c % 2 + 1) * D] = part
+                    scores[i * 4 + c // 2, h, :, (c % 2) * D : (c % 2 + 1) * D] = part
                     best = jnp.maximum(best, part)
                 peak[h] = best
                 return 0
@@ -226,85 +225,84 @@
             peak[h] = best
             return 0
 
-        lax.fori_loop(0, PER, diagonal, 0, unroll=True)
-        lax.fori_loop(0, BACK // 2, pair, 0)
-
-    def out_copy(head, d):
+        if lo == 0:
+            lax.fori_loop(0, PER, diagonal, 0, unroll=True)
+        lax.fori_loop(lo, hi, pair, 0)
+
+    def out_lanes(two):
+        return pl.ds(pl.multiple_of((z * 8 + two) * 2 * D, 2 * D), 2 * D)
+
+    def out_copy(two, d):
         to = (z + d) % N_KV
         return pltpu.make_async_remote_copy(
-            src_ref=obuf.at[head, pl.ds(to * 64, 64), :],
-            dst_ref=out_ref.at[:, pl.ds(pl.multiple_of((z * 16 + head) * D, D), D)],
+            src_ref=obuf.at[two, pl.ds(to * 64, 64), :],
+            dst_ref=out_ref.at[:, out_lanes(two)],
             send_sem=osend.at[0],
             recv_sem=orecv.at[0],
             device_id={"kv": to},
             device_id_type=MESH,
         )
 
-    def pass2(g, hooks):
+    def pass2(g, lo, hi):
         values = jnp.concatenate([tile(2 * g + 1, i) for i in range(BACK + 1)], axis=0)
 
-        def head(h, _):
-            hooks(h)
-            top = jnp.max(peak[h], axis=1, keepdims=True)
-            wide = jnp.broadcast_to(top, (T, D))
-            total = jnp.zeros((T, D), F32)
-            probs = []
-            for i in range(BACK + 1):
-                for c in range(2):
-                    p = jnp.exp2((scores[i, h, :, c * D : (c + 1) * D] - wide) * C2)
-                    total = total + p
-                    probs.append(p.astype(BF))
+        def pair(k, _):
+            probs, tops, sums = [], [], []
+            for e in range(2):
+                h = 2 * k + e
+                top = jnp.max(peak[h], axis=1, keepdims=True)
+                wide = jnp.broadcast_to(top, (T, D))
+                total = jnp.zeros((T, D), F32)
+                parts = []
+                for i in range(BACK + 1):
+                    for c in range(2):
+                        p = jnp.exp2((scores[i, h, :, c * D : (c + 1) * D] - wide) * C2)
+                        total = total + p
+                        parts.append(p.astype(BF))
+                probs.append(jnp.concatenate(parts, axis=1))
+                tops.append(top)
+                sums.append(jnp.sum(total, axis=1, keepdims=True))
             mixed = jnp.dot(
-                jnp.concatenate(probs, axis=1), values, preferred_element_type=F32
+                jnp.concatenate(probs, axis=0), values, preferred_element_type=F32
             )
-            row_sum = jnp.sum(total, axis=1, keepdims=True)
-            here = g * PER + h
-            obuf[here] = (mixed / row_sum).astype(BF)
-            norm = top * SCALE + jnp.log(row_sum)
-            lse_own[...] = jnp.where(lane == here, norm, lse_own[...])
+            here = g * (PER // 2) + k
+            norms = lse_own[...]
+            for e in range(2):
+                part = mixed[e * T : (e + 1) * T] / sums[e]
+                obuf[here, :, e * D : (e + 1) * D] = part.astype(BF)
+                norms = jnp.where(lane == 2 * here + e, tops[e] * SCALE + jnp.log(sums[e]), norms)
+            lse_own[...] = norms
             for d in range(1, N_KV):
                 out_copy(here, d).start()
-            out_ref[:, pl.ds(pl.multiple_of((z * 16 + here) * D, D), D)] = obuf[
-                here, pl.ds(pl.multiple_of(z * 64, 64), 64), :
-            ]
+            out_ref[:, out_lanes(here)] = obuf[here, pl.ds(pl.multiple_of(z * 64, 64), 64), :]
             return 0
 
-        lax.fori_loop(0, PER, head, 0)
+        lax.fori_loop(lo, hi, pair, 0)
 
     lse_own[...] = jnp.zeros((T, D), F32)
-    def hooks_of(table):
-        def hooks(k):
-            for step, calls in table.items():
-
-                @pl.when(k == step)
-                def _():
-                    for call, *where in calls:
-                        call(*where)
-
-        return hooks
-
-    pass1(0, hooks_of({
-        0: [(stage_a, 2)],
-        1: [(stage_t, 1, 2), (stage_t, 1, 1)],
-        2: [(stage_t, 1, 0)],
-        4: [(settle, 0, 0), (stage_b, 2)],
-        6: [(stage_a, 3)],
-    }))
+    stage_a(2)
+    stage_a(3)
+    pass1(0, 0, 2)
+    stage_t(1, 2)
+    stage_t(1, 1)
+    settle(0, 0)
+    pass1(0, 2, 4)
+    stage_t(1, 0)
+    stage_b(2)
+    stage_b(3)
     for row in range(3):
         settle(1, row)
-    pass2(0, hooks_of({
-        0: [(stage_t, 2, 2), (stage_t, 2, 1)],
-        1: [(stage_t, 2, 0)],
-        2: [(stage_b, 3)],
-        5: [(stage_t, 3, 2), (stage_t, 3, 1)],
-        6: [(stage_t, 3, 0)],
-    }))
+    pass2(0, 0, 4)
+    for row in (2, 1, 0):
+        stage_t(2, row)
+    for row in (2, 1, 0):
+        stage_t(3, row)
     for row in range(3):
         settle(2, row)
-    pass1(1, lambda k: None)
+    pass1(1, 0, 4)
     for row in range(3):
         settle(3, row)
-    pass2(1, lambda h: None)
+    pass2(1, 0, 4)
 
     spread_rows = (
         lax.broadcasted_iota(jnp.int32, (T, N_TOK), 0) // 8
@@ -351,7 +349,7 @@
     finish(lse_recv.at[pl.ds(0, N_TOK - 1)], lrecv)
     lse_ref[...] = lse_recv[...].reshape(T, D).T[:16, :]
     finish(lse_send.at[pl.ds(0, N_TOK - 1)], lsend)
-    finish(obuf.at[pl.ds(0, 12)], osend)
+    finish(obuf.at[pl.ds(0, 6)], osend)
     finish(out_ref.at[:, pl.ds(0, 48 * D)], orecv)
 
 
@@ -363,8 +361,8 @@
     return pl.pallas_call(
         kernel,
         out_shape=(
-            jax.ShapeDtypeStruct((T // N_KV, N_KV * GROUPS * PER * D), BF),
-            jax.ShapeDtypeStruct((GROUPS * PER, T), F32),
+            pltpu.VMEM((T // N_KV, N_KV * GROUPS * PER * D), BF),
+            pltpu.VMEM((GROUPS * PER, T), F32),
         ),
         in_specs=[pl.BlockSpec(memory_space=pltpu.SMEM)] + [vmem] * 2 + [far] * 3,
         out_specs=(vmem, vmem),
@@ -376,7 +374,7 @@
             pltpu.VMEM((GROUPS * PER, T, D), BF),
             pltpu.VMEM((BACK + 1, PER, T, T), F32),
             pltpu.VMEM((PER, T, D), F32),
-            pltpu.VMEM((GROUPS * PER, T, D), BF),
+            pltpu.VMEM((GROUPS * PER // 2, T, 2 * D), BF),
             pltpu.VMEM((T, D), jnp.int32),
             pltpu.VMEM((T, D), F32),
             pltpu.VMEM((T, D), F32),
@@ -393,7 +391,7 @@
             pltpu.SemaphoreType.DMA((1,)),
         ],
         compiler_params=pltpu.CompilerParams(
-            collective_id=0, has_side_effects=True, vmem_limit_bytes=60 << 20
+            collective_id=0, has_side_effects=True, vmem_limit_bytes=58 << 20
         ),
     )(doc_lengths, freq, block_plan, queries, key_states, value_states)
 

time: 71.7 us -> 65.9 us (0.919)
  Pallas kernels: 68 us -> 63.5 us
  local copies, waits for them, and re-layouts: 2.88 us -> 1.58 us
    pallas_call x1, Pallas kernels: 68 us -> 63.5 us  [body(): pl.pallas_call(kernel, out_shape=(pltpu.VMEM((T // N_KV, N_KV * GROUPS *...]
    unnamed x4 -> x2, local copies, waits for them, and re-layouts: 2.88 us -> 1.58 us
where the time goes in v4:
time: 65.9 us; the launch traced here: 65.7 us
  Pallas kernels  63.5 us (96%)
  local copies, waits for them, and re-layouts  1.58 us (2%)
    pallas_call x1, Pallas kernels, body(): pl.pallas_call(kernel, out_shape=(pltpu.VMEM((T // N_KV, N_KV * GROUPS *...  63.5 us
    unnamed x2, local copies, waits for them, and re-layouts  1.58 us

profile of v4, /device:TPU:1, one launch (start us, length us, event | category | flops | bytes accessed | tf_op | source)
XLA Modules:
  0.0 65.7 jit_solution(15460517789271913707)
XLA Ops:
  0.6 63.5 %shard_map.77 = (bf16[64,8192]{1,0:T(8,128)(2,1)S(1)}, f32[16,256]{1,0:T(8,128)S(1)}) custom-call(s32[16]{0:T(128)} %doc_ref.1, f32[1,128]{1,0:T(1,128)} %constant.2.clone.freq_ref, s32[32,32]{1,0:T(8,128)} %plan_ref.1, bf16[256,2048]{1,0:T(8,128)(2,1)} %q_hbm.1, bf16[256,256]{1,0:T(8,128)(2,1)} %k_hbm.1, bf16[256,256]{1,0:T(8,128)(2,1)} %v_hbm.1), custom_call_target="tpu_custom_call" | custom-call | tf_op jit(solution)/shard_map/pallas_call | solution.py:361
  64.1 1.0 %copy.10 = bf16[64,8192]{1,0:T(8,128)(2,1)} copy(bf16[64,8192]{1,0:T(8,128)(2,1)S(1)} %get-tuple-element.2) | data formatting | bytes 2097152
  65.1 0.6 copy.11

commit v5 on v4

--- a/solution.py
+++ b/solution.py
@@ -165,19 +165,6 @@
         qrot[h] = rotate(q_ref[:, lanes])
         return 0
 
-    stage_a(0)
-    loads[2].wait()
-    lax.fori_loop(0, PER, turn, 0)
-    stage_b(0)
-    stage_a(1)
-    lax.fori_loop(PER, 2 * PER, turn, 0)
-    stage_t(0, 2)
-    stage_t(0, 1)
-    stage_b(1)
-    stage_t(0, 0)
-    settle(0, 2)
-    settle(0, 1)
-
     def tile(t, i):
         at = pos + i
         place = at % 8
@@ -210,6 +197,9 @@
             lax.fori_loop(0, PER, head, 0, unroll=True)
             return 0
 
+        lax.fori_loop(lo, hi, pair, 0)
+
+    def pass1_own(g):
         keys = tile(2 * g, BACK)
 
         def diagonal(h, _):
@@ -225,9 +215,7 @@
             peak[h] = best
             return 0
 
-        if lo == 0:
-            lax.fori_loop(0, PER, diagonal, 0, unroll=True)
-        lax.fori_loop(lo, hi, pair, 0)
+        lax.fori_loop(0, PER, diagonal, 0, unroll=True)
 
     def out_lanes(two):
         return pl.ds(pl.multiple_of((z * 8 + two) * 2 * D, 2 * D), 2 * D)
@@ -245,32 +233,31 @@
 
     def pass2(g, lo, hi):
         values = jnp.concatenate([tile(2 * g + 1, i) for i in range(BACK + 1)], axis=0)
+        values = jnp.concatenate([values, jnp.ones_like(values)], axis=1)
 
         def pair(k, _):
-            probs, tops, sums = [], [], []
+            probs, tops = [], []
             for e in range(2):
                 h = 2 * k + e
                 top = jnp.max(peak[h], axis=1, keepdims=True)
                 wide = jnp.broadcast_to(top, (T, D))
-                total = jnp.zeros((T, D), F32)
                 parts = []
                 for i in range(BACK + 1):
                     for c in range(2):
                         p = jnp.exp2((scores[i, h, :, c * D : (c + 1) * D] - wide) * C2)
-                        total = total + p
                         parts.append(p.astype(BF))
                 probs.append(jnp.concatenate(parts, axis=1))
                 tops.append(top)
-                sums.append(jnp.sum(total, axis=1, keepdims=True))
             mixed = jnp.dot(
                 jnp.concatenate(probs, axis=0), values, preferred_element_type=F32
             )
             here = g * (PER // 2) + k
             norms = lse_own[...]
             for e in range(2):
-                part = mixed[e * T : (e + 1) * T] / sums[e]
+                row_sum = mixed[e * T : (e + 1) * T, D:]
+                part = mixed[e * T : (e + 1) * T, :D] / row_sum
                 obuf[here, :, e * D : (e + 1) * D] = part.astype(BF)
-                norms = jnp.where(lane == 2 * here + e, tops[e] * SCALE + jnp.log(sums[e]), norms)
+                norms = jnp.where(lane == 2 * here + e, tops[e] * SCALE + jnp.log(row_sum), norms)
             lse_own[...] = norms
             for d in range(1, N_KV):
                 out_copy(here, d).start()
@@ -280,26 +267,43 @@
         lax.fori_loop(lo, hi, pair, 0)
 
     lse_own[...] = jnp.zeros((T, D), F32)
+    stage_a(0)
+    loads[2].wait()
+    lax.fori_loop(0, PER, turn, 0)
+    stage_b(0)
+    stage_a(1)
+    pass1_own(0)
+    lax.fori_loop(PER, 2 * PER, turn, 0)
+    stage_t(0, 2)
+    stage_t(0, 1)
+    stage_b(1)
+    stage_t(0, 0)
+    settle(0, 2)
+    settle(0, 1)
     stage_a(2)
     stage_a(3)
     pass1(0, 0, 2)
     stage_t(1, 2)
     stage_t(1, 1)
     settle(0, 0)
-    pass1(0, 2, 4)
+    pass1(0, 2, 3)
     stage_t(1, 0)
     stage_b(2)
-    stage_b(3)
+    pass1(0, 3, 4)
     for row in range(3):
         settle(1, row)
-    pass2(0, 0, 4)
+    stage_b(3)
+    pass2(0, 0, 3)
     for row in (2, 1, 0):
         stage_t(2, row)
+    pass2(0, 3, 4)
+    for row in range(3):
+        settle(2, row)
+    pass1_own(1)
+    pass1(1, 0, 2)
     for row in (2, 1, 0):
         stage_t(3, row)
-    for row in range(3):
-        settle(2, row)
-    pass1(1, 0, 4)
+    pass1(1, 2, 4)
     for row in range(3):
         settle(3, row)
     pass2(1, 0, 4)

time: 65.9 us -> 57.8 us (0.88)
  Pallas kernels: 63.5 us -> 55.4 us
    pallas_call x1, Pallas kernels: 63.5 us -> 55.4 us  [body(): pl.pallas_call(kernel, out_shape=(pltpu.VMEM((T // N_KV, N_KV * GROUPS *...]
where the time goes in v5:
time: 57.8 us; the launch traced here: 57.6 us
  Pallas kernels  55.4 us (96%)
  local copies, waits for them, and re-layouts  1.58 us (3%)
  between operations  0.64 us (1%)
    pallas_call x1, Pallas kernels, body(): pl.pallas_call(kernel, out_shape=(pltpu.VMEM((T // N_KV, N_KV * GROUPS *...  55.4 us
    unnamed x2, local copies, waits for them, and re-layouts  1.58 us

profile of v5, /device:TPU:1, one launch (start us, length us, event | category | flops | bytes accessed | tf_op | source)
XLA Modules:
  0.0 57.6 jit_solution(11807567917794832150)
XLA Ops:
  0.6 55.4 %shard_map.77 = (bf16[64,8192]{1,0:T(8,128)(2,1)S(1)}, f32[16,256]{1,0:T(8,128)S(1)}) custom-call(s32[16]{0:T(128)} %doc_ref.1, f32[1,128]{1,0:T(1,128)} %constant.2.clone.freq_ref, s32[32,32]{1,0:T(8,128)} %plan_ref.1, bf16[256,2048]{1,0:T(8,128)(2,1)} %q_hbm.1, bf16[256,256]{1,0:T(8,128)(2,1)} %k_hbm.1, bf16[256,256]{1,0:T(8,128)(2,1)} %v_hbm.1), custom_call_target="tpu_custom_call" | custom-call | tf_op jit(solution)/shard_map/pallas_call | solution.py:365
  56.1 1.0 %copy.10 = bf16[64,8192]{1,0:T(8,128)(2,1)} copy(bf16[64,8192]{1,0:T(8,128)(2,1)S(1)} %get-tuple-element.2) | data formatting | bytes 2097152
  57.0 0.6 %copy.11 = f32[16,256]{1,0:T(8,128)} copy(f32[16,256]{1,0:T(8,128)S(1)} %get-tuple-element.3) | data formatting | bytes 32768

commit v6 on v5

--- a/solution.py
+++ b/solution.py
@@ -281,29 +281,29 @@
     settle(0, 2)
     settle(0, 1)
     stage_a(2)
-    stage_a(3)
     pass1(0, 0, 2)
     stage_t(1, 2)
     stage_t(1, 1)
     settle(0, 0)
+    stage_b(2)
     pass1(0, 2, 3)
     stage_t(1, 0)
-    stage_b(2)
+    stage_a(3)
     pass1(0, 3, 4)
     for row in range(3):
         settle(1, row)
-    stage_b(3)
-    pass2(0, 0, 3)
+    pass2(0, 0, 1)
     for row in (2, 1, 0):
         stage_t(2, row)
-    pass2(0, 3, 4)
+    stage_b(3)
+    pass2(0, 1, 4)
     for row in range(3):
         settle(2, row)
     pass1_own(1)
-    pass1(1, 0, 2)
+    pass1(1, 0, 1)
     for row in (2, 1, 0):
         stage_t(3, row)
-    pass1(1, 2, 4)
+    pass1(1, 1, 4)
     for row in range(3):
         settle(3, row)
     pass2(1, 0, 4)

time: 57.8 us -> 55.8 us (0.965)
  Pallas kernels: 55.4 us -> 53.4 us
    pallas_call x1, Pallas kernels: 55.4 us -> 53.4 us  [body(): pl.pallas_call(kernel, out_shape=(pltpu.VMEM((T // N_KV, N_KV * GROUPS *...]
where the time goes in v6:
time: 55.8 us; the launch traced here: 55.6 us
  Pallas kernels  53.4 us (96%)
  local copies, waits for them, and re-layouts  1.58 us (3%)
  between operations  0.64 us (1%)
    pallas_call x1, Pallas kernels, body(): pl.pallas_call(kernel, out_shape=(pltpu.VMEM((T // N_KV, N_KV * GROUPS *...  53.4 us
    unnamed x2, local copies, waits for them, and re-layouts  1.58 us

profile of v6, /device:TPU:1, one launch (start us, length us, event | category | flops | bytes accessed | tf_op | source)
XLA Modules:
  0.0 55.6 jit_solution(4632689216143652962)
XLA Ops:
  0.6 53.4 %shard_map.77 = (bf16[64,8192]{1,0:T(8,128)(2,1)S(1)}, f32[16,256]{1,0:T(8,128)S(1)}) custom-call(s32[16]{0:T(128)} %doc_ref.1, f32[1,128]{1,0:T(1,128)} %constant.2.clone.freq_ref, s32[32,32]{1,0:T(8,128)} %plan_ref.1, bf16[256,2048]{1,0:T(8,128)(2,1)} %q_hbm.1, bf16[256,256]{1,0:T(8,128)(2,1)} %k_hbm.1, bf16[256,256]{1,0:T(8,128)(2,1)} %v_hbm.1), custom_call_target="tpu_custom_call" | custom-call | tf_op jit(solution)/shard_map/pallas_call | solution.py:365
  54.1 1.0 %copy.10 = bf16[64,8192]{1,0:T(8,128)(2,1)} copy(bf16[64,8192]{1,0:T(8,128)(2,1)S(1)} %get-tuple-element.2) | data formatting | bytes 2097152
  55.0 0.6 %copy.11 = f32[16,256]{1,0:T(8,128)} copy(f32[16,256]{1,0:T(8,128)S(1)} %get-tuple-element.3) | data formatting | bytes 32768

commit v7 on v6

--- a/solution.py
+++ b/solution.py
@@ -272,9 +272,9 @@
     lax.fori_loop(0, PER, turn, 0)
     stage_b(0)
     stage_a(1)
-    pass1_own(0)
     lax.fori_loop(PER, 2 * PER, turn, 0)
     stage_t(0, 2)
+    pass1_own(0)
     stage_t(0, 1)
     stage_b(1)
     stage_t(0, 0)

time: 55.8 us -> 55.8 us (level)
  no operation moved by 1% of the time
where the time goes in v7:
time: 55.8 us; the launch traced here: 55.6 us
  Pallas kernels  53.4 us (96%)
  local copies, waits for them, and re-layouts  1.58 us (3%)
  between operations  0.64 us (1%)
    pallas_call x1, Pallas kernels, body(): pl.pallas_call(kernel, out_shape=(pltpu.VMEM((T // N_KV, N_KV * GROUPS *...  53.4 us
    unnamed x2, local copies, waits for them, and re-layouts  1.58 us

profile of v7, /device:TPU:1, one launch (start us, length us, event | category | flops | bytes accessed | tf_op | source)
XLA Modules:
  0.0 55.6 jit_solution(9516872015047197552)
XLA Ops:
  0.6 53.4 %shard_map.77 = (bf16[64,8192]{1,0:T(8,128)(2,1)S(1)}, f32[16,256]{1,0:T(8,128)S(1)}) custom-call(s32[16]{0:T(128)} %doc_ref.1, f32[1,128]{1,0:T(1,128)} %constant.2.clone.freq_ref, s32[32,32]{1,0:T(8,128)} %plan_ref.1, bf16[256,2048]{1,0:T(8,128)(2,1)} %q_hbm.1, bf16[256,256]{1,0:T(8,128)(2,1)} %k_hbm.1, bf16[256,256]{1,0:T(8,128)(2,1)} %v_hbm.1), custom_call_target="tpu_custom_call" | custom-call | tf_op jit(solution)/shard_map/pallas_call | solution.py:365
  54.0 1.0 %copy.10 = bf16[64,8192]{1,0:T(8,128)(2,1)} copy(bf16[64,8192]{1,0:T(8,128)(2,1)S(1)} %get-tuple-element.2) | data formatting | bytes 2097152
  55.0 0.6 %copy.11 = f32[16,256]{1,0:T(8,128)} copy(f32[16,256]{1,0:T(8,128)S(1)} %get-tuple-element.3) | data formatting | bytes 32768
